TPU v7x, 32 devices: a whole 2x2x4 slice. The times are simulated.
32 devices in a mesh: freq: 2 (over x), grp: 4 (over z), sub: 4 (over y, core).
Axes of the slice: x: 2, y: 2, z: 4, core: 2. Of those that a mesh axis runs over, the one named last changes fastest.
Arguments:
- alm: bfloat16 [256, 16, 2, 1024], P('freq', ('grp', 'sub')), may hold values from -6 to 6
- band_index: int32 [32, 32], replicated, may hold values from 0 to 255
- band_weight: float32 [32, 32], replicated, may hold values from 0.05 to 0.5
- legendre: bfloat16 [16, 1024, 1024], P(('grp', 'sub')), may hold values from -0.03125 to 0.03125
- orders: int32 [16], replicated, may hold values from 0 to 1023, as said below
- owner: int32 [32768, 1], P(('grp', 'sub')), may hold values from 0 to 15; in each aligned block of 2048 rows (0 to 2047, 2048 to 4095, ...) at most 192 rows name the same one
- tile_local: int32 [32768], P(('grp', 'sub')), may hold values from 0 to 127
- interp: bfloat16 [32768, 512], P(('grp', 'sub')), may hold values from -0.25 to 0.25
Outputs:
- tod: bfloat16 [32768, 32], P(('grp', 'sub'), 'freq')
Inputs may be any that keep to these rules, and one draw needn't show every extreme that they name: 16 distinct orders; 0 and 1023 are always among them. `owner`: among the 2048 samples of one index of grp and sub (aligned blocks of 2048 rows) no cycle band is named more than 192 times, a bound that some block reaches.
All inputs are finite; a program needn't handle non-finite values.
Results may differ from a plain program's by a relative error of at most 0.0073.
Values may be sent and summed in bfloat16 or wider, within the bound.
No kernel may reach another device: no remote copies, remote signals or barrier semaphores. Data moves between devices by JAX's collectives and lax.ppermute only.
A program may use at most 64 MiB of HBM per device.

v0:
```python
import functools
import math

import jax
import jax.numpy as jnp
from jax import lax
from jax.experimental import pallas as pl
from jax.experimental.pallas import tpu as pltpu
from jax.sharding import PartitionSpec as P


NPHI = 1024
TR = 4
TPHI = 128
LANES = 128
LOWS = LANES // (2 * TR)
FOLD = 4
SMALL = 12 * 2**20
F32 = jnp.float32
BF16 = jnp.bfloat16
CONTRACT_LAST = (((1,), (1,)), ((), ()))


def iota(shape, axis):
    return lax.broadcasted_iota(jnp.int32, shape, axis)


def in_hbm(value):
    return pltpu.with_memory_space_constraint(value, pltpu.HBM)


def band_kernel(
    tiles_each, slots,
    index_ref, weight_ref, orders_ref, owner_ref, tile_ref, alm_ref,
    own_ref, send_ref, lanes_ref, code_ref,
    index, weight, orders, owner, tile, alm, sem
):
    sources = (index_ref, weight_ref, orders_ref, alm_ref, owner_ref, tile_ref)
    copies = [
        pltpu.make_async_copy(source, target, sem.at[n])
        for n, (source, target) in enumerate(zip(sources, (index, weight, orders, alm, owner, tile)))
    ]
    for copy in copies:
        copy.start()
    freqs, _, multipoles = alm.shape
    rows = 2 * freqs
    dets, entries = index.shape
    half = dets // 2
    me = lax.axis_index("freq")
    slot = lax.axis_index("grp") * lax.axis_size("sub") + lax.axis_index("sub")
    column = iota((dets, rows), 1)
    wanted = me * freqs + lax.shift_right_logical(column, 1)
    band = jnp.zeros((dets, rows), F32)
    copies[0].wait()
    copies[1].wait()
    for k in range(entries):
        hit = index[:, k : k + 1] == wanted
        band = band + jnp.where(hit, weight[:, k : k + 1], 0.0)
    part = lax.bitwise_and(column[:half], 1)
    low, high = band[:half], band[half:]
    own = jnp.where(me == 0, low, high)
    other = jnp.where(me == 0, high, low)
    matrix = jnp.concatenate(
        [jnp.where(part == c, side, 0.0) for side in (own, other) for c in range(2)]
    ).astype(BF16)
    copies[2].wait()
    keep = iota((dets, multipoles), 1) >= orders[slot]
    lane = iota(lanes_ref.shape, 1)
    held = lane_order(lane)
    order = jnp.zeros(lanes_ref.shape, jnp.int32)
    for j, here in enumerate(slots(slot)):
        order = jnp.where(held == j, orders[here], order)
    lanes_ref[...] = order
    copies[4].wait()
    copies[5].wait()
    code_ref[...] = owner[...] * tiles_each + tile[...]
    copies[3].wait()
    table = alm[...].reshape(rows, multipoles)
    sums = jnp.dot(matrix, table, preferred_element_type=F32)
    own_ref[...] = jnp.where(keep, sums[:dets], 0.0)
    send_ref[...] = jnp.where(keep, sums[dets:], 0.0).astype(BF16)


def lane_order(lane):
    half = LANES // 2
    return lane % (half // TR) // 2 + LOWS // 2 * (lane % LANES // half)


def band_sums(band_index, band_weight, orders, owner, tile, alm, tiles_each, slots):
    multipoles = alm.shape[2]
    dets = band_index.shape[0]
    lines = (owner.shape[0] // LANES, LANES)
    operands = (band_index, band_weight, orders, owner.reshape(lines), tile.reshape(lines), alm)
    return pl.pallas_call(
        functools.partial(band_kernel, tiles_each, slots),
        out_shape=(
            jax.ShapeDtypeStruct((dets, multipoles), F32),
            jax.ShapeDtypeStruct((dets, multipoles), BF16),
            jax.ShapeDtypeStruct((8, 2 * LANES), jnp.int32),
            jax.ShapeDtypeStruct(lines, jnp.int32),
        ),
        in_specs=[pl.BlockSpec(memory_space=pltpu.HBM)] * len(operands),
        scratch_shapes=[
            pltpu.VMEM(band_index.shape, jnp.int32),
            pltpu.VMEM(band_weight.shape, F32),
            pltpu.SMEM(orders.shape, jnp.int32),
            pltpu.VMEM(lines, jnp.int32),
            pltpu.VMEM(lines, jnp.int32),
            pltpu.VMEM(alm.shape, BF16),
            pltpu.SemaphoreType.DMA((len(operands),)),
        ],
        compiler_params=pltpu.CompilerParams(vmem_limit_bytes=SMALL),
        name="band_sums",
    )(*[in_hbm(value) for value in operands])


def cycle_kernel(own_ref, recv_ref, legendre_ref, out_ref):
    rows = own_ref.shape[0]
    half = rows // 2
    cycles = legendre_ref.shape[1]
    coefs = (own_ref[...] + recv_ref[...].astype(F32)).astype(BF16)
    table = jnp.dot(coefs, legendre_ref[...], preferred_element_type=F32)
    first = iota((half, LANES), 1) < LANES // 2
    lines = []
    for tile in range(cycles // LANES):
        both = table[:, tile * LANES : (tile + 1) * LANES]
        turned = pltpu.roll(both, LANES // 2, 1)
        lines.append(jnp.where(first, both[:half], turned[half:]))
        lines.append(jnp.where(first, turned[:half], both[half:]))
    each = LANES // half
    for block in range(len(lines) // each):
        square = jnp.concatenate(lines[block * each : (block + 1) * each])
        out_ref[:, block * LANES : (block + 1) * LANES] = square.T.astype(BF16)


def cycle_coefs(own, received, legendre):
    rows, _ = own.shape
    cycles = legendre.shape[1]
    return pl.pallas_call(
        cycle_kernel,
        out_shape=jax.ShapeDtypeStruct((LANES, rows * cycles // LANES), BF16),
        in_specs=[pl.BlockSpec(memory_space=pltpu.VMEM)] * 3,
        compiler_params=pltpu.CompilerParams(vmem_limit_bytes=SMALL),
        name="cycle_coefs",
    )(own, received, legendre)


def copy_table(first_row):
    parts = LANES // 2 // TR
    row = iota((LANES, FOLD * LANES // 2), 0) - first_row
    lane = iota((LANES, FOLD * LANES // 2), 1)
    hit = (row >= 0) & (row < LANES // 2)
    hit = hit & (row // parts == lane % TR) & (row % parts == lane // (FOLD * TR))
    return jnp.where(hit, 1.0, 0.0).astype(BF16)


def column_of(line):
    return jnp.broadcast_to(line.astype(F32), (LANES, LANES)).T


def lane_bits(rows):
    return (iota((rows, LANES), 1) // TR) % FOLD


def spread_kernel(
    lanes_ref, code_ref, interp_hbm, near_ref, far_ref, base_ref, turn_ref, interp_ref, sem
):
    samples, _ = interp_ref.shape
    lon_tiles = NPHI // TPHI
    rows = min(512, samples)
    copies = []
    for step in range(samples // rows):
        here = pl.ds(step * rows, rows)
        copies.append(
            pltpu.make_async_copy(interp_hbm.at[here, :], interp_ref.at[here, :], sem.at[step])
        )
        copies[-1].start()

    place = iota((TPHI, 2 * LANES), 0)
    lane = iota((TPHI, 2 * LANES), 1)
    side = lane // LANES
    order = jnp.broadcast_to(lanes_ref[:1, :], (TPHI, 2 * LANES))
    turns = order * place + (NPHI // 4) * (side + lane % 2)
    angle = lax.bitwise_and(turns, NPHI - 1).astype(F32) * (2.0 * math.pi / NPHI)
    base = jnp.where(order == 0, 1.0, 2.0) * jnp.cos(angle)
    for i in range(TR):
        kept = jnp.where(lane % (LANES // 2) // (LANES // 2 // TR) == i, base, 0.0)
        base_ref[i * TPHI : (i + 1) * TPHI, :] = kept.astype(BF16)
    few = 2 * lon_tiles
    place, side, order = place[:few], side[:few], order[:few]
    turns = order * (place % lon_tiles) * TPHI + 3 * (NPHI // 4) * side
    angle = lax.bitwise_and(turns, NPHI - 1).astype(F32) * (2.0 * math.pi / NPHI)
    turn = jnp.cos(angle)
    rounded = turn.astype(BF16).astype(F32)
    turn = jnp.where(place < lon_tiles, rounded, turn - rounded)
    turn_ref[...] = jnp.zeros(turn_ref.shape, BF16)
    turn_ref[:few, :] = turn.astype(BF16)

    code = code_ref[...]
    lon_tile = lax.bitwise_and(code, lon_tiles - 1).astype(F32)
    cycle_tile = lax.shift_right_logical(code, lon_tiles.bit_length() - 1)
    low = lax.bitwise_and(cycle_tile, LOWS - 1).astype(F32).astype(BF16)
    high = lax.shift_right_logical(cycle_tile, LOWS.bit_length() - 1).astype(F32).astype(BF16)
    lines = samples // LANES
    for packet in (near_ref, far_ref):
        packet[samples // 2 : samples // 2 + lines, :] = low
        packet[samples // 2 + lines :, :] = high

    lane = iota((rows, LANES), 1)
    tile_of_lane = jnp.where(lane < few, lane % lon_tiles, -1).astype(F32)
    first = lane < LANES // 2
    before = []
    for step in range(samples // rows):
        groups = range(step * rows // LANES, (step + 1) * rows // LANES)
        columns = jnp.concatenate([column_of(lon_tile[g : g + 1, :]) for g in groups])
        tile_hit = jnp.where(columns == tile_of_lane, 1.0, 0.0).astype(BF16)
        turn = jnp.dot(tile_hit, turn_ref[...], preferred_element_type=F32)
        copies[step].wait()
        here = slice(step * rows, (step + 1) * rows)
        pair = jnp.dot(interp_ref[here, :], base_ref[...], preferred_element_type=F32) * turn
        both = pair[:, :LANES] + pair[:, LANES:]
        if step < samples // rows // 2:
            before.append(both)
            continue
        step -= samples // rows // 2
        here = slice(step * rows, (step + 1) * rows)
        swapped = pltpu.roll(both, LANES // 2, 1)
        near_ref[here, :] = jnp.where(first, before[step], swapped).astype(BF16)
        swapped = pltpu.roll(before[step], LANES // 2, 1)
        far_ref[here, :] = jnp.where(first, swapped, both).astype(BF16)


def spread_samples(order_lanes, code, interp):
    samples, pixels = interp.shape
    lines = samples // LANES
    packet = jax.ShapeDtypeStruct((samples // 2 + 2 * lines, LANES), BF16)
    return pl.pallas_call(
        spread_kernel,
        out_shape=(packet, packet),
        in_specs=[pl.BlockSpec(memory_space=pltpu.VMEM)] * 2
        + [pl.BlockSpec(memory_space=pltpu.HBM)],
        scratch_shapes=[
            pltpu.VMEM((pixels, 2 * LANES), BF16),
            pltpu.VMEM((LANES, 2 * LANES), BF16),
            pltpu.VMEM((samples, pixels), BF16),
            pltpu.SemaphoreType.DMA((samples // min(512, samples),)),
        ],
        compiler_params=pltpu.CompilerParams(vmem_limit_bytes=SMALL),
        name="spread_samples",
        cost_estimate=pl.CostEstimate(
            flops=samples * pixels * LANES * 16,
            bytes_accessed=samples * pixels * 4,
            transcendentals=0,
        ),
    )(order_lanes, code, in_hbm(interp))


def unpack_kernel(packet_ref, x_ref, low_ref, high_ref):
    samples = x_ref.shape[0]
    lines = samples // LANES
    rows = min(512, samples // 2)
    half = samples // 2
    for side in range(2):
        copy = copy_table(side * LANES // 2)
        for step in range(half // rows):
            part = packet_ref[step * rows : (step + 1) * rows, :]
            spread = jnp.dot(part, copy, preferred_element_type=F32)
            x_ref[side * half + step * rows : side * half + (step + 1) * rows, :] = spread.astype(BF16)
    low = packet_ref[half : half + lines, :].astype(F32)
    high = packet_ref[half + lines :, :].astype(F32)
    bits = lane_bits(LANES).astype(F32)
    for g in range(lines):
        here = slice(g * LANES, (g + 1) * LANES)
        low_ref[here, :] = (column_of(low[g : g + 1, :]) - bits).astype(BF16)
        high_ref[here, :] = column_of(high[g : g + 1, :]).astype(BF16)


def unpack_samples(packet, samples):
    return pl.pallas_call(
        unpack_kernel,
        out_shape=(
            jax.ShapeDtypeStruct((samples, FOLD * LANES // 2), BF16),
            jax.ShapeDtypeStruct((samples, LANES), BF16),
            jax.ShapeDtypeStruct((samples, LANES), BF16),
        ),
        in_specs=[pl.BlockSpec(memory_space=pltpu.VMEM)],
        compiler_params=pltpu.CompilerParams(vmem_limit_bytes=SMALL),
        name="unpack_samples",
        cost_estimate=pl.CostEstimate(
            flops=samples * LANES * LANES * 8, bytes_accessed=samples * LANES * 8, transcendentals=0
        ),
    )(packet)


def pick_kernel(counts, first_block, more, last, x_ref, low_ref, high_ref, *refs):
    stacks, rest = refs[: len(counts)], refs[len(counts) :]
    sums_ref = rest[0] if more else None
    out_ref, table_ref = rest[-2], rest[-1]
    samples = x_ref.shape[0]
    wide = table_ref.shape[1]
    steps, tile = LOWS // FOLD, FOLD * TR
    blocks = sum(counts) // (LANES // (2 * tile))
    j = 0
    for stack, count in zip(stacks, counts):
        for k in range(count):
            for c in range(2):
                for q in range(steps):
                    table_ref[pl.ds(q * blocks * LANES + (2 * j + c) * tile, tile), :] = stack[
                        pl.ds(k * LANES + (c * steps + q) * tile, tile), :
                    ]
            j += 1

    rows = min(512, samples)
    zero = jnp.zeros((rows, LANES), BF16)
    for step in range(samples // rows):
        here = slice(step * rows, (step + 1) * rows)
        low = low_ref[here, :]
        cut = [
            jnp.where(
                low == jnp.asarray(FOLD * q, BF16),
                x_ref[here, (first_block + b) * LANES : (first_block + b + 1) * LANES],
                zero,
            )
            for q in range(steps)
            for b in range(blocks)
        ]
        sums = jnp.dot(
            jnp.concatenate(cut, axis=1), table_ref[...], preferred_element_type=F32
        )
        if more:
            sums = sums + sums_ref[here, :]
        if not last:
            out_ref[here, :] = sums
            continue
        dets = out_ref.shape[0]
        sums = sums.astype(BF16)
        kept = []
        for b in range(wide // LANES):
            lane = ((iota((rows, LANES), 1) + LANES * b) // dets).astype(F32).astype(BF16)
            hit = high_ref[here, :] == lane
            kept.append(jnp.where(hit, sums[:, b * LANES : (b + 1) * LANES], zero))
        gather = iota((dets, wide), 1) % dets == iota((dets, wide), 0)
        gather = jnp.where(gather, 1.0, 0.0).astype(BF16)
        out_ref[:, here] = lax.dot_general(
            gather, jnp.concatenate(kept, axis=1), CONTRACT_LAST, preferred_element_type=F32
        ).astype(BF16)


def pick_values(x, low, high, stacks, first, sums, dets):
    samples = x.shape[0]
    counts = tuple(stack.shape[0] // LANES for stack in stacks)
    wide = stacks[0].shape[1]
    more = [] if sums is None else [sums]
    operands = [x, low, high, *stacks, *more]
    shape = ((samples, wide), F32) if dets is None else ((dets, samples), BF16)
    return pl.pallas_call(
        functools.partial(
            pick_kernel, counts, first * 2 * FOLD * TR // LANES, bool(more), dets is not None
        ),
        out_shape=jax.ShapeDtypeStruct(*shape),
        in_specs=[pl.BlockSpec(memory_space=pltpu.VMEM)] * len(operands),
        scratch_shapes=[pltpu.VMEM((sum(counts) * LANES, wide), BF16)],
        compiler_params=pltpu.CompilerParams(vmem_limit_bytes=16 * 2**20),
        name="pick_values",
        cost_estimate=pl.CostEstimate(
            flops=samples * sum(counts) * LANES * wide * 2, bytes_accessed=samples * 2048, transcendentals=0
        ),
    )(*operands)


def swap(value, axis, step):
    size = lax.axis_size(axis)
    return lax.ppermute(value, axis, [(i, i ^ step) for i in range(size)])


def in_chunks(piece, orders, code, interp, dets):
    chunks = orders.shape[0] // LOWS
    lanes = piece.shape[1]
    steps = LOWS // FOLD
    samples = interp.shape[0]
    gathered = lax.all_gather(piece, ("grp", "sub"), axis=0)
    gathered = gathered.reshape(chunks, LOWS, 2, steps, FOLD * TR, lanes)
    held = lane_order(iota((8, 2 * LANES), 1))

    def add_chunk(member, sums):
        packets = spread_samples(orders[member * LOWS + held], code, interp)
        near, far = [unpack_samples(packet, samples) for packet in packets]
        x, low = jnp.concatenate([near[0], far[0]], axis=1), near[1]
        table = lax.dynamic_index_in_dim(gathered, member, 0, False)
        table = table.transpose(2, 0, 1, 3, 4).reshape(steps, FOLD * LANES, lanes)
        for q in range(steps):
            hit = jnp.tile(low == FOLD * q, (1, FOLD))
            cut = jnp.where(hit, x, jnp.zeros_like(x))
            sums = sums + jnp.dot(cut, table[q], preferred_element_type=F32)
        return sums

    sums = lax.fori_loop(0, chunks, add_chunk, jnp.zeros((samples, lanes), F32))
    mark = code.reshape(-1) // ((NPHI // TPHI) * LOWS)
    hit = mark[:, None] == lax.iota(jnp.int32, lanes // dets)[None, :]
    sums = sums.reshape(samples, lanes // dets, dets)
    return jnp.sum(jnp.where(hit[:, :, None], sums, 0.0), axis=1).astype(BF16)


def on_device(alm, band_index, band_weight, legendre, orders, owner, tile_local, interp):
    group_count = lax.axis_size("grp")
    sub_count = lax.axis_size("sub")
    local_freqs = alm.shape[0]
    multipoles = alm.shape[3]
    cycles = legendre.shape[2]
    dets = band_weight.shape[0] // lax.axis_size("freq")
    samples = interp.shape[0]
    tiles_each = (cycles // (group_count * sub_count) // TR) * (NPHI // TPHI)
    far = sub_count // 2

    def slots(mine):
        return [
            (mine // sub_count ^ g) * sub_count + (mine % sub_count ^ s)
            for s in range(sub_count)
            for g in range(group_count)
        ][:LOWS]

    own, send, order_lanes, code = band_sums(
        band_index,
        band_weight,
        orders,
        owner[:, 0],
        tile_local,
        alm.reshape(local_freqs, 2, multipoles),
        tiles_each,
        slots,
    )
    received = swap(send, "freq", 1)
    if orders.shape[0] != LOWS:
        piece = cycle_coefs(own, received, legendre[0])
        return in_chunks(piece, orders, code, interp, dets)

    near_packet, far_packet = spread_samples(order_lanes, code, interp)
    got = swap(far_packet, "sub", far)
    received, near_packet = lax.optimization_barrier((received, near_packet))
    piece = cycle_coefs(own, received, legendre[0])
    gathered = [swap(piece, "grp", g) for g in range(1, group_count)]
    near_packet, _ = lax.optimization_barrier((near_packet, piece))
    near_x = unpack_samples(near_packet, samples)
    far_x = unpack_samples(got, samples)
    gathered, near_x, far_x = lax.optimization_barrier((gathered, near_x, far_x))
    stack = jnp.concatenate([piece] + gathered)
    stacks = [stack] + [swap(stack, "sub", s) for s in range(1, far)]
    sums = pick_values(*far_x, stacks[:1], 0, None, None)
    far_values = pick_values(*far_x, stacks[1:], group_count, sums, dets)
    other = swap(far_values, "sub", far)
    values = pick_values(*near_x, stacks, 0, None, dets)
    return (values.astype(F32) + other.astype(F32)).astype(BF16).T


def solution(mesh):
    placed = (
        P("freq", ("grp", "sub"), None, None),
        P(),
        P(),
        P(("grp", "sub"), None, None),
        P(),
        P(("grp", "sub"), None),
        P(("grp", "sub")),
        P(("grp", "sub"), None),
    )

    return jax.shard_map(
        on_device, mesh=mesh, in_specs=placed, out_specs=P(("grp", "sub"), "freq"), check_vma=False
    )
```

profile of v0, /device:TPU:0, one launch (start us, length us, event | category | flops | bytes accessed | tf_op | source)
XLA Modules:
  0.0 30.0 jit_solution(16172516688306595095)
XLA Ops:
  0.0 1.4 %band_sums.1 = (f32[32,1024]{1,0:T(8,128)S(1)}, bf16[32,1024]{1,0:T(8,128)(2,1)S(1)}, s32[8,256]{1,0:T(8,128)S(1)}, s32[16,128]{1,0:T(8,128)S(1)}) custom-call(s32[32,32]{1,0:T(8,128)} %index_ref.1, f32[32,32]{1,0:T(8,128)} %weight_ref.1, s32[16]{0:T(128)} %orders_ref.1, s32[16,128]{1,0:T(8,128)} %bitcast.8, s32[16,128]{1,0:T(8,128)} %bitcast.9, ...), custom_call_target="tpu_custom_call" | custom-call | tf_op jit(solution)/shard_map/band_sums/pallas_call | solution.py:94
  1.4 0.0 copy-start
  1.5 3.3 %spread_samples.1 = (bf16[1056,128]{1,0:T(8,128)(2,1)S(1)}, bf16[1056,128]{1,0:T(8,128)(2,1)S(1)}) custom-call(s32[8,256]{1,0:T(8,128)S(1)} %get-tuple-element.31.lanes_ref, s32[16,128]{1,0:T(8,128)S(1)} %get-tuple-element.32.code_ref, bf16[2048,512]{1,0:T(8,128)(2,1)} %interp_hbm.1), custom_call_target="tpu_custom_call" | custom-call | flops 2147483648 | bytes 4194304 | tf_op jit(solution)/shard_map/spread_samples/pallas_call | solution.py:237
  4.8 3.1 %collective-permute-start.4 = (bf16[1056,128]{1,0:T(8,128)(2,1)S(1)}, bf16[1056,128]{1,0:T(8,128)(2,1)S(1)}, u32[]{:S(2)}, u32[]{:S(2)}) collective-permute-start(bf16[1056,128]{1,0:T(8,128)(2,1)S(1)} %get-tuple-element.40), channel_id=1, source_target_pairs={{0,2},{1,3},{2,0},{3,1},{4,6},{5,7},{6,4},{7,5},{8,10},{9,11},{10,... | collective-permute-start | bytes 811016 | tf_op jit(solution)/shard_map/ppermute | solution.py:373
  7.8 1.5 %collective-permute-start = (bf16[32,1024]{1,0:T(8,128)(2,1)S(1)}, bf16[32,1024]{1,0:T(8,128)(2,1)S(1)}, u32[]{:S(2)}, u32[]{:S(2)}) collective-permute-start(bf16[32,1024]{1,0:T(8,128)(2,1)S(1)} %get-tuple-element.30), channel_id=1, source_target_pairs={{0,16},{16,0},{1,17},{17,1},{2,18},{18,2},{3,19},{19,3},{4,20},{20... | collective-permute-start | bytes 196616 | tf_op jit(solution)/shard_map/ppermute | solution.py:373
  9.3 2.8 %collective-permute-done.recv_ref = bf16[32,1024]{1,0:T(8,128)(2,1)S(1)} collective-permute-done((bf16[32,1024]{1,0:T(8,128)(2,1)S(1)}, bf16[32,1024]{1,0:T(8,128)(2,1)S(1)}, u32[]{:S(2)}, u32[]{:S(2)}) %collective-permute-start) | collective-permute-done | bytes 65568 | tf_op jit(solution)/shard_map/ppermute | solution.py:373
  12.1 0.6 %cycle_coefs.1 = bf16[128,256]{1,0:T(8,128)(2,1)S(1)} custom-call(f32[32,1024]{1,0:T(8,128)S(1)} %get-tuple-element.29.own_ref, bf16[32,1024]{1,0:T(8,128)(2,1)S(1)} %collective-permute-done.recv_ref, bf16[1024,1024]{1,0:T(8,128)(2,1)S(1)} %bitcast.6), custom_call_target="tpu_custom_call" | custom-call | tf_op jit(solution)/shard_map/cycle_coefs/pallas_call | solution.py:139
  12.8 3.7 %collective-permute-start.3 = (bf16[128,256]{1,0:T(8,128)(2,1)S(1)}, bf16[128,256]{1,0:T(8,128)(2,1)S(1)}, u32[]{:S(2)}, u32[]{:S(2)}) collective-permute-start(bf16[128,256]{1,0:T(8,128)(2,1)S(1)} %cycle_coefs.1), channel_id=1, source_target_pairs={{0,12},{4,8},{8,4},{12,0},{1,13},{5,9},{9,5},{13,1},{2,14},{6,10},... | collective-permute-start | bytes 196616 | tf_op jit(solution)/shard_map/ppermute | solution.py:373
  16.4 0.0 collective-permute-start.2
  16.4 0.8 %collective-permute-start.1 = (bf16[128,256]{1,0:T(8,128)(2,1)S(1)}, bf16[128,256]{1,0:T(8,128)(2,1)S(1)}, u32[]{:S(2)}, u32[]{:S(2)}) collective-permute-start(bf16[128,256]{1,0:T(8,128)(2,1)S(1)} %cycle_coefs.1), channel_id=1, source_target_pairs={{0,4},{4,0},{8,12},{12,8},{1,5},{5,1},{9,13},{13,9},{2,6},{6,2},{1... | collective-permute-start | bytes 196616 | tf_op jit(solution)/shard_map/ppermute | solution.py:373
  17.2 0.5 %unpack_samples.2 = (bf16[2048,256]{1,0:T(8,128)(2,1)S(1)}, bf16[2048,128]{1,0:T(8,128)(2,1)S(1)}, bf16[2048,128]{1,0:T(8,128)(2,1)S(1)}) custom-call(bf16[1056,128]{1,0:T(8,128)(2,1)S(1)} %get-tuple-element.36.packet_ref), custom_call_target="tpu_custom_call" | custom-call | flops 268435456 | bytes 2097152 | tf_op jit(solution)/shard_map/unpack_samples/pallas_call | solution.py:279
  17.7 0.0 collective-permute-done.4.packet_ref
  17.7 0.5 %unpack_samples.3 = (bf16[2048,256]{1,0:T(8,128)(2,1)S(1)}, bf16[2048,128]{1,0:T(8,128)(2,1)S(1)}, bf16[2048,128]{1,0:T(8,128)(2,1)S(1)}) custom-call(bf16[1056,128]{1,0:T(8,128)(2,1)S(1)} %collective-permute-done.4.packet_ref), custom_call_target="tpu_custom_call" | custom-call | flops 268435456 | bytes 2097152 | tf_op jit(solution)/shard_map/unpack_samples/pallas_call | solution.py:279
  18.3 0.6 %collective-permute-done.3 = bf16[128,256]{1,0:T(8,128)(2,1)S(1)} collective-permute-done((bf16[128,256]{1,0:T(8,128)(2,1)S(1)}, bf16[128,256]{1,0:T(8,128)(2,1)S(1)}, u32[]{:S(2)}, u32[]{:S(2)}) %collective-permute-start.3) | collective-permute-done | bytes 65568 | tf_op jit(solution)/shard_map/ppermute | solution.py:373
  18.9 2.7 %collective-permute-done.2 = bf16[128,256]{1,0:T(8,128)(2,1)S(1)} collective-permute-done((bf16[128,256]{1,0:T(8,128)(2,1)S(1)}, bf16[128,256]{1,0:T(8,128)(2,1)S(1)}, u32[]{:S(2)}, u32[]{:S(2)}) %collective-permute-start.2) | collective-permute-done | bytes 65568 | tf_op jit(solution)/shard_map/ppermute | solution.py:373
  21.6 0.0 collective-permute-done.1
  21.7 0.1 collective-permute-start.5
  21.7 0.7 %pick_values.4.refs_1_ = f32[2048,256]{1,0:T(8,128)S(1)} custom-call(bf16[2048,256]{1,0:T(8,128)(2,1)S(1)} %get-tuple-element.50.x_ref, bf16[2048,128]{1,0:T(8,128)(2,1)S(1)} %get-tuple-element.51.low_ref, bf16[2048,128]{1,0:T(8,128)(2,1)S(1)} %get-tuple-element.52.high_ref, bf16[512,256]{1,0:T(8,128)(2,1)S(1)} %pad_maximum_fusion.refs_0_), custom_call_target="tpu_custom_call" | custom-call | flops 536870912 | bytes 4194304 | tf_op jit(solution)/shard_map/pick_values/pallas_call | solution.py:356
  22.5 0.8 %collective-permute-done.5.refs_1_.refs_0_ = bf16[512,256]{1,0:T(8,128)(2,1)S(1)} collective-permute-done((bf16[512,256]{1,0:T(8,128)(2,1)S(1)}, bf16[512,256]{1,0:T(8,128)(2,1)S(1)}, u32[]{:S(2)}, u32[]{:S(2)}) %collective-permute-start.5) | collective-permute-done | bytes 262176 | tf_op jit(solution)/shard_map/ppermute | solution.py:373
  23.3 1.8 %pick_values.5 = bf16[16,2048]{1,0:T(8,128)(2,1)S(1)} custom-call(bf16[2048,256]{1,0:T(8,128)(2,1)S(1)} %get-tuple-element.50.x_ref, bf16[2048,128]{1,0:T(8,128)(2,1)S(1)} %get-tuple-element.51.low_ref, bf16[2048,128]{1,0:T(8,128)(2,1)S(1)} %get-tuple-element.52.high_ref, bf16[512,256]{1,0:T(8,128)(2,1)S(1)} %collective-permute-done.5.refs_1_.refs_0_, ...), custom_call_target="tpu_custom_call" | custom-call | flops 536870912 | bytes 4194304 | tf_op jit(solution)/shard_map/pick_values/pallas_call | solution.py:356
  25.1 0.5 %collective-permute-start.6 = (bf16[16,2048]{1,0:T(8,128)(2,1)S(1)}, bf16[16,2048]{1,0:T(8,128)(2,1)S(1)}, u32[]{:S(2)}, u32[]{:S(2)}) collective-permute-start(bf16[16,2048]{1,0:T(8,128)(2,1)S(1)} %pick_values.5), channel_id=1, source_target_pairs={{0,2},{1,3},{2,0},{3,1},{4,6},{5,7},{6,4},{7,5},{8,10},{9,11},{10,... | collective-permute-start | bytes 196616 | tf_op jit(solution)/shard_map/ppermute | solution.py:373
  25.6 2.9 %pick_values.3 = bf16[16,2048]{1,0:T(8,128)(2,1)S(1)} custom-call(bf16[2048,256]{1,0:T(8,128)(2,1)S(1)} %get-tuple-element.44.x_ref, bf16[2048,128]{1,0:T(8,128)(2,1)S(1)} %get-tuple-element.45.low_ref, bf16[2048,128]{1,0:T(8,128)(2,1)S(1)} %get-tuple-element.46.high_ref, bf16[512,256]{1,0:T(8,128)(2,1)S(1)} %pad_maximum_fusion.refs_0_, ...), custom_call_target="tpu_custom_call" | custom-call | flops 1073741824 | bytes 4194304 | tf_op jit(solution)/shard_map/pick_values/pallas_call | solution.py:356
  28.4 0.9 %collective-permute-done.6 = bf16[16,2048]{1,0:T(8,128)(2,1)S(1)} collective-permute-done((bf16[16,2048]{1,0:T(8,128)(2,1)S(1)}, bf16[16,2048]{1,0:T(8,128)(2,1)S(1)}, u32[]{:S(2)}, u32[]{:S(2)}) %collective-permute-start.6) | collective-permute-done | bytes 65568 | tf_op jit(solution)/shard_map/ppermute | solution.py:373
  29.3 0.6 %fusion = bf16[2048,16]{0,1:T(8,128)(2,1)} fusion(bf16[16,2048]{1,0:T(8,128)(2,1)S(1)} %collective-permute-done.6, bf16[16,2048]{1,0:T(8,128)(2,1)S(1)} %pick_values.3), kind=kLoop, calls=%fused_computation.2 | loop fusion | flops 131072 | bytes 196608 | tf_op jit(solution)/shard_map/transpose | solution.py:452
  (2 shorter events, 0.0 us)
Async XLA Ops:
  1.4 10.7 %copy-start = (bf16[1,1024,1024]{2,1,0:T(8,128)(2,1)S(1)}, bf16[1,1024,1024]{2,1,0:T(8,128)(2,1)}, u32[]{:S(2)}) copy-start(bf16[1,1024,1024]{2,1,0:T(8,128)(2,1)} %param.11) | copy-start | bytes 6291460
  4.8 12.9 %collective-permute-start.4 = (bf16[1056,128]{1,0:T(8,128)(2,1)S(1)}, bf16[1056,128]{1,0:T(8,128)(2,1)S(1)}, u32[]{:S(2)}, u32[]{:S(2)}) collective-permute-start(bf16[1056,128]{1,0:T(8,128)(2,1)S(1)} %get-tuple-element.40), channel_id=1, source_target_pairs={{0,2},{1,3},{2,0},{3,1},{4,6},{5,7},{6,4},{7,5},{8,10},{9,11},{10,... | collective-permute-start | bytes 811016 | tf_op jit(solution)/shard_map/ppermute | solution.py:373
  7.8 4.3 %collective-permute-start = (bf16[32,1024]{1,0:T(8,128)(2,1)S(1)}, bf16[32,1024]{1,0:T(8,128)(2,1)S(1)}, u32[]{:S(2)}, u32[]{:S(2)}) collective-permute-start(bf16[32,1024]{1,0:T(8,128)(2,1)S(1)} %get-tuple-element.30), channel_id=1, source_target_pairs={{0,16},{16,0},{1,17},{17,1},{2,18},{18,2},{3,19},{19,3},{4,20},{20... | collective-permute-start | bytes 196616 | tf_op jit(solution)/shard_map/ppermute | solution.py:373
  12.8 6.1 %collective-permute-start.3 = (bf16[128,256]{1,0:T(8,128)(2,1)S(1)}, bf16[128,256]{1,0:T(8,128)(2,1)S(1)}, u32[]{:S(2)}, u32[]{:S(2)}) collective-permute-start(bf16[128,256]{1,0:T(8,128)(2,1)S(1)} %cycle_coefs.1), channel_id=1, source_target_pairs={{0,12},{4,8},{8,4},{12,0},{1,13},{5,9},{9,5},{13,1},{2,14},{6,10},... | collective-permute-start | bytes 196616 | tf_op jit(solution)/shard_map/ppermute | solution.py:373
  16.4 5.2 %collective-permute-start.2 = (bf16[128,256]{1,0:T(8,128)(2,1)S(1)}, bf16[128,256]{1,0:T(8,128)(2,1)S(1)}, u32[]{:S(2)}, u32[]{:S(2)}) collective-permute-start(bf16[128,256]{1,0:T(8,128)(2,1)S(1)} %cycle_coefs.1), channel_id=1, source_target_pairs={{0,8},{4,12},{8,0},{12,4},{1,9},{5,13},{9,1},{13,5},{2,10},{6,14},... | collective-permute-start | bytes 196616 | tf_op jit(solution)/shard_map/ppermute | solution.py:373
  16.4 5.2 %collective-permute-start.1 = (bf16[128,256]{1,0:T(8,128)(2,1)S(1)}, bf16[128,256]{1,0:T(8,128)(2,1)S(1)}, u32[]{:S(2)}, u32[]{:S(2)}) collective-permute-start(bf16[128,256]{1,0:T(8,128)(2,1)S(1)} %cycle_coefs.1), channel_id=1, source_target_pairs={{0,4},{4,0},{8,12},{12,8},{1,5},{5,1},{9,13},{13,9},{2,6},{6,2},{1... | collective-permute-start | bytes 196616 | tf_op jit(solution)/shard_map/ppermute | solution.py:373
  21.7 1.6 %collective-permute-start.5 = (bf16[512,256]{1,0:T(8,128)(2,1)S(1)}, bf16[512,256]{1,0:T(8,128)(2,1)S(1)}, u32[]{:S(2)}, u32[]{:S(2)}) collective-permute-start(bf16[512,256]{1,0:T(8,128)(2,1)S(1)} %pad_maximum_fusion.refs_0_), channel_id=1, source_target_pairs={{0,1},{1,0},{2,3},{3,2},{4,5},{5,4},{6,7},{7,6},{8,9},{9,8},{10,11... | collective-permute-start | bytes 786440 | tf_op jit(solution)/shard_map/ppermute | solution.py:373
  25.1 4.3 %collective-permute-start.6 = (bf16[16,2048]{1,0:T(8,128)(2,1)S(1)}, bf16[16,2048]{1,0:T(8,128)(2,1)S(1)}, u32[]{:S(2)}, u32[]{:S(2)}) collective-permute-start(bf16[16,2048]{1,0:T(8,128)(2,1)S(1)} %pick_values.5), channel_id=1, source_target_pairs={{0,2},{1,3},{2,0},{3,1},{4,6},{5,7},{6,4},{7,5},{8,10},{9,11},{10,... | collective-permute-start | bytes 196616 | tf_op jit(solution)/shard_map/ppermute | solution.py:373
where the time goes:
time: 30.2 us; the launch traced here: 30 us
  Pallas kernels  11.8 us (39%)
  starting transfers between devices  9.55 us (32%)
  waiting for transfers between devices  7.85 us (26%)
  other arithmetic  0.67 us (2%)
    ppermute x7, starting transfers between devices, swap(): return lax.ppermute(value, axis, [(i, i ^ step) for i in range(size)])  9.55 us
    ppermute x7, waiting for transfers between devices, swap(): return lax.ppermute(value, axis, [(i, i ^ step) for i in range(size)])  7.85 us
    pallas_call x3, Pallas kernels, pick_values(): pl.pallas_call(functools.partial(pick_kernel, counts, first * 2 * FOLD *...  5.42 us
    pallas_call x1, Pallas kernels, spread_samples(): pl.pallas_call(spread_kernel, out_shape=(packet, packet), in_specs=[pl.Bl...  3.32 us
    pallas_call x1, Pallas kernels, band_sums(): pl.pallas_call(functools.partial(band_kernel, tiles_each, slots), out_sha...  1.44 us
    pallas_call x2, Pallas kernels, unpack_samples(): pl.pallas_call(unpack_kernel, out_shape=(jax.ShapeDtypeStruct((samples, F...  1.02 us
    transpose x1, other arithmetic, on_device(): return (values.astype(F32) + other.astype(F32)).astype(BF16).T  0.65 us
    pallas_call x1, Pallas kernels, cycle_coefs(): pl.pallas_call(cycle_kernel, out_shape=jax.ShapeDtypeStruct((LANES, rows...  0.64 us
  transfers between devices with their start and end apart: 7, of which 5 were waited for; matrix products, arithmetic and copies ran while one was open for 0% of the time, Pallas kernels for 18%

commit v1 on v0

--- a/solution.py
+++ b/solution.py
@@ -295,9 +295,8 @@
 def pick_kernel(counts, first_block, more, last, x_ref, low_ref, high_ref, *refs):
     stacks, rest = refs[: len(counts)], refs[len(counts) :]
     sums_ref = rest[0] if more else None
-    out_ref, table_ref = rest[-2], rest[-1]
+    out_ref, table_ref, held_ref = rest[-3:]
     samples = x_ref.shape[0]
-    wide = table_ref.shape[1]
     steps, tile = LOWS // FOLD, FOLD * TR
     blocks = sum(counts) // (LANES // (2 * tile))
     j = 0
@@ -329,21 +328,36 @@
         )
         if more:
             sums = sums + sums_ref[here, :]
-        if not last:
+        if last:
+            held_ref[here, :] = sums
+        else:
             out_ref[here, :] = sums
-            continue
-        dets = out_ref.shape[0]
-        sums = sums.astype(BF16)
+    if last:
+        finish(held_ref, high_ref, out_ref, ())
+
+
+def finish(sums_ref, high_ref, out_ref, more):
+    samples, wide = sums_ref.shape
+    dets = out_ref.shape[0]
+    rows = min(512, samples)
+    gather = iota((dets, wide), 1) % dets == iota((dets, wide), 0)
+    gather = jnp.where(gather, 1.0, 0.0).astype(BF16)
+    lanes = [
+        ((iota((rows, LANES), 1) + LANES * b) // dets).astype(F32).astype(BF16)
+        for b in range(wide // LANES)
+    ]
+    for step in range(samples // rows):
+        here = slice(step * rows, (step + 1) * rows)
         kept = []
-        for b in range(wide // LANES):
-            lane = ((iota((rows, LANES), 1) + LANES * b) // dets).astype(F32).astype(BF16)
-            hit = high_ref[here, :] == lane
-            kept.append(jnp.where(hit, sums[:, b * LANES : (b + 1) * LANES], zero))
-        gather = iota((dets, wide), 1) % dets == iota((dets, wide), 0)
-        gather = jnp.where(gather, 1.0, 0.0).astype(BF16)
-        out_ref[:, here] = lax.dot_general(
+        for b, lane in enumerate(lanes):
+            part = sums_ref[here, b * LANES : (b + 1) * LANES].astype(BF16)
+            kept.append(jnp.where(high_ref[here, :] == lane, part, jnp.zeros_like(part)))
+        values = lax.dot_general(
             gather, jnp.concatenate(kept, axis=1), CONTRACT_LAST, preferred_element_type=F32
-        ).astype(BF16)
+        )
+        for other in more:
+            values = values + other[:, here].astype(F32)
+        out_ref[:, here] = values.astype(BF16)
 
 
 def pick_values(x, low, high, stacks, first, sums, dets):
@@ -359,7 +373,10 @@
         ),
         out_shape=jax.ShapeDtypeStruct(*shape),
         in_specs=[pl.BlockSpec(memory_space=pltpu.VMEM)] * len(operands),
-        scratch_shapes=[pltpu.VMEM((sum(counts) * LANES, wide), BF16)],
+        scratch_shapes=[
+            pltpu.VMEM((sum(counts) * LANES, wide), BF16),
+            pltpu.VMEM((8 if dets is None else samples, wide), F32),
+        ],
         compiler_params=pltpu.CompilerParams(vmem_limit_bytes=16 * 2**20),
         name="pick_values",
         cost_estimate=pl.CostEstimate(

time: 30.2 us -> 29.5 us (0.977)
  Pallas kernels: 11.8 us -> 9.69 us
  waiting for transfers between devices: 7.85 us -> 9.24 us
    pallas_call x3, Pallas kernels: 5.42 us -> 3.27 us  [pick_values(): pl.pallas_call(functools.partial(pick_kernel, counts, first * 2 * FOLD *...]
    ppermute x7, waiting for transfers between devices: 7.85 us -> 9.24 us  [swap(): return lax.ppermute(value, axis, [(i, i ^ step) for i in range(size)])]
  transfers between devices with their start and end apart: 7 -> 7, of which waited for: 5 -> 5; matrix products, arithmetic and copies ran while one was open for 0% -> 0% of each run, Pallas kernels for 18% -> 13%
where the time goes in v1:
time: 29.5 us; the launch traced here: 29.2 us
  Pallas kernels  9.69 us (33%)
  starting transfers between devices  9.56 us (32%)
  waiting for transfers between devices  9.24 us (31%)
  other arithmetic  0.67 us (2%)
    ppermute x7, starting transfers between devices, swap(): return lax.ppermute(value, axis, [(i, i ^ step) for i in range(size)])  9.56 us
    ppermute x7, waiting for transfers between devices, swap(): return lax.ppermute(value, axis, [(i, i ^ step) for i in range(size)])  9.24 us
    pallas_call x1, Pallas kernels, spread_samples(): pl.pallas_call(spread_kernel, out_shape=(packet, packet), in_specs=[pl.Bl...  3.32 us
    pallas_call x3, Pallas kernels, pick_values(): pl.pallas_call(functools.partial(pick_kernel, counts, first * 2 * FOLD *...  3.27 us
    pallas_call x1, Pallas kernels, band_sums(): pl.pallas_call(functools.partial(band_kernel, tiles_each, slots), out_sha...  1.44 us
    pallas_call x2, Pallas kernels, unpack_samples(): pl.pallas_call(unpack_kernel, out_shape=(jax.ShapeDtypeStruct((samples, F...  1.02 us
    transpose x1, other arithmetic, on_device(): return (values.astype(F32) + other.astype(F32)).astype(BF16).T  0.65 us
    pallas_call x1, Pallas kernels, cycle_coefs(): pl.pallas_call(cycle_kernel, out_shape=jax.ShapeDtypeStruct((LANES, rows...  0.64 us
  transfers between devices with their start and end apart: 7, of which 5 were waited for; matrix products, arithmetic and copies ran while one was open for 0% of the time, Pallas kernels for 13%

profile of v1, /device:TPU:0, one launch (start us, length us, event | category | flops | bytes accessed | tf_op | source)
XLA Modules:
  0.0 29.2 jit_solution(16568073486380197603)
XLA Ops:
  0.0 1.4 %band_sums.1 = (f32[32,1024]{1,0:T(8,128)S(1)}, bf16[32,1024]{1,0:T(8,128)(2,1)S(1)}, s32[8,256]{1,0:T(8,128)S(1)}, s32[16,128]{1,0:T(8,128)S(1)}) custom-call(s32[32,32]{1,0:T(8,128)} %index_ref.1, f32[32,32]{1,0:T(8,128)} %weight_ref.1, s32[16]{0:T(128)} %orders_ref.1, s32[16,128]{1,0:T(8,128)} %bitcast.8, s32[16,128]{1,0:T(8,128)} %bitcast.9, ...), custom_call_target="tpu_custom_call" | custom-call | tf_op jit(solution)/shard_map/band_sums/pallas_call | solution.py:94
  1.4 0.0 copy-start
  1.5 3.3 %spread_samples.1 = (bf16[1056,128]{1,0:T(8,128)(2,1)S(1)}, bf16[1056,128]{1,0:T(8,128)(2,1)S(1)}) custom-call(s32[8,256]{1,0:T(8,128)S(1)} %get-tuple-element.31.lanes_ref, s32[16,128]{1,0:T(8,128)S(1)} %get-tuple-element.32.code_ref, bf16[2048,512]{1,0:T(8,128)(2,1)} %interp_hbm.1), custom_call_target="tpu_custom_call" | custom-call | flops 2147483648 | bytes 4194304 | tf_op jit(solution)/shard_map/spread_samples/pallas_call | solution.py:237
  4.8 3.1 %collective-permute-start.4 = (bf16[1056,128]{1,0:T(8,128)(2,1)S(1)}, bf16[1056,128]{1,0:T(8,128)(2,1)S(1)}, u32[]{:S(2)}, u32[]{:S(2)}) collective-permute-start(bf16[1056,128]{1,0:T(8,128)(2,1)S(1)} %get-tuple-element.40), channel_id=1, source_target_pairs={{0,2},{1,3},{2,0},{3,1},{4,6},{5,7},{6,4},{7,5},{8,10},{9,11},{10,... | collective-permute-start | bytes 811016 | tf_op jit(solution)/shard_map/ppermute | solution.py:390
  7.8 1.5 %collective-permute-start = (bf16[32,1024]{1,0:T(8,128)(2,1)S(1)}, bf16[32,1024]{1,0:T(8,128)(2,1)S(1)}, u32[]{:S(2)}, u32[]{:S(2)}) collective-permute-start(bf16[32,1024]{1,0:T(8,128)(2,1)S(1)} %get-tuple-element.30), channel_id=1, source_target_pairs={{0,16},{16,0},{1,17},{17,1},{2,18},{18,2},{3,19},{19,3},{4,20},{20... | collective-permute-start | bytes 196616 | tf_op jit(solution)/shard_map/ppermute | solution.py:390
  9.3 2.8 %collective-permute-done.recv_ref = bf16[32,1024]{1,0:T(8,128)(2,1)S(1)} collective-permute-done((bf16[32,1024]{1,0:T(8,128)(2,1)S(1)}, bf16[32,1024]{1,0:T(8,128)(2,1)S(1)}, u32[]{:S(2)}, u32[]{:S(2)}) %collective-permute-start) | collective-permute-done | bytes 65568 | tf_op jit(solution)/shard_map/ppermute | solution.py:390
  12.1 0.6 %cycle_coefs.1 = bf16[128,256]{1,0:T(8,128)(2,1)S(1)} custom-call(f32[32,1024]{1,0:T(8,128)S(1)} %get-tuple-element.29.own_ref, bf16[32,1024]{1,0:T(8,128)(2,1)S(1)} %collective-permute-done.recv_ref, bf16[1024,1024]{1,0:T(8,128)(2,1)S(1)} %bitcast.6), custom_call_target="tpu_custom_call" | custom-call | tf_op jit(solution)/shard_map/cycle_coefs/pallas_call | solution.py:139
  12.8 3.7 %collective-permute-start.3 = (bf16[128,256]{1,0:T(8,128)(2,1)S(1)}, bf16[128,256]{1,0:T(8,128)(2,1)S(1)}, u32[]{:S(2)}, u32[]{:S(2)}) collective-permute-start(bf16[128,256]{1,0:T(8,128)(2,1)S(1)} %cycle_coefs.1), channel_id=1, source_target_pairs={{0,12},{4,8},{8,4},{12,0},{1,13},{5,9},{9,5},{13,1},{2,14},{6,10},... | collective-permute-start | bytes 196616 | tf_op jit(solution)/shard_map/ppermute | solution.py:390
  16.4 0.0 collective-permute-start.2
  16.4 0.8 %collective-permute-start.1 = (bf16[128,256]{1,0:T(8,128)(2,1)S(1)}, bf16[128,256]{1,0:T(8,128)(2,1)S(1)}, u32[]{:S(2)}, u32[]{:S(2)}) collective-permute-start(bf16[128,256]{1,0:T(8,128)(2,1)S(1)} %cycle_coefs.1), channel_id=1, source_target_pairs={{0,4},{4,0},{8,12},{12,8},{1,5},{5,1},{9,13},{13,9},{2,6},{6,2},{1... | collective-permute-start | bytes 196616 | tf_op jit(solution)/shard_map/ppermute | solution.py:390
  17.2 0.5 %unpack_samples.2 = (bf16[2048,256]{1,0:T(8,128)(2,1)S(1)}, bf16[2048,128]{1,0:T(8,128)(2,1)S(1)}, bf16[2048,128]{1,0:T(8,128)(2,1)S(1)}) custom-call(bf16[1056,128]{1,0:T(8,128)(2,1)S(1)} %get-tuple-element.36.packet_ref), custom_call_target="tpu_custom_call" | custom-call | flops 268435456 | bytes 2097152 | tf_op jit(solution)/shard_map/unpack_samples/pallas_call | solution.py:279
  17.7 0.0 collective-permute-done.4.packet_ref
  17.7 0.5 %unpack_samples.3 = (bf16[2048,256]{1,0:T(8,128)(2,1)S(1)}, bf16[2048,128]{1,0:T(8,128)(2,1)S(1)}, bf16[2048,128]{1,0:T(8,128)(2,1)S(1)}) custom-call(bf16[1056,128]{1,0:T(8,128)(2,1)S(1)} %collective-permute-done.4.packet_ref), custom_call_target="tpu_custom_call" | custom-call | flops 268435456 | bytes 2097152 | tf_op jit(solution)/shard_map/unpack_samples/pallas_call | solution.py:279
  18.3 0.6 %collective-permute-done.3 = bf16[128,256]{1,0:T(8,128)(2,1)S(1)} collective-permute-done((bf16[128,256]{1,0:T(8,128)(2,1)S(1)}, bf16[128,256]{1,0:T(8,128)(2,1)S(1)}, u32[]{:S(2)}, u32[]{:S(2)}) %collective-permute-start.3) | collective-permute-done | bytes 65568 | tf_op jit(solution)/shard_map/ppermute | solution.py:390
  18.9 2.7 %collective-permute-done.2 = bf16[128,256]{1,0:T(8,128)(2,1)S(1)} collective-permute-done((bf16[128,256]{1,0:T(8,128)(2,1)S(1)}, bf16[128,256]{1,0:T(8,128)(2,1)S(1)}, u32[]{:S(2)}, u32[]{:S(2)}) %collective-permute-start.2) | collective-permute-done | bytes 65568 | tf_op jit(solution)/shard_map/ppermute | solution.py:390
  21.6 0.0 collective-permute-done.1
  21.7 0.1 collective-permute-start.5
  21.7 0.7 %pick_values.4.refs_1_ = f32[2048,256]{1,0:T(8,128)S(1)} custom-call(bf16[2048,256]{1,0:T(8,128)(2,1)S(1)} %get-tuple-element.50.x_ref, bf16[2048,128]{1,0:T(8,128)(2,1)S(1)} %get-tuple-element.51.low_ref, bf16[2048,128]{1,0:T(8,128)(2,1)S(1)} %get-tuple-element.52.high_ref, bf16[512,256]{1,0:T(8,128)(2,1)S(1)} %pad_maximum_fusion.refs_0_), custom_call_target="tpu_custom_call" | custom-call | flops 536870912 | bytes 4194304 | tf_op jit(solution)/shard_map/pick_values/pallas_call | solution.py:370
  22.5 0.8 %collective-permute-done.5.refs_1_.refs_0_ = bf16[512,256]{1,0:T(8,128)(2,1)S(1)} collective-permute-done((bf16[512,256]{1,0:T(8,128)(2,1)S(1)}, bf16[512,256]{1,0:T(8,128)(2,1)S(1)}, u32[]{:S(2)}, u32[]{:S(2)}) %collective-permute-start.5) | collective-permute-done | bytes 262176 | tf_op jit(solution)/shard_map/ppermute | solution.py:390
  23.3 1.0 %pick_values.5 = bf16[16,2048]{1,0:T(8,128)(2,1)S(1)} custom-call(bf16[2048,256]{1,0:T(8,128)(2,1)S(1)} %get-tuple-element.50.x_ref, bf16[2048,128]{1,0:T(8,128)(2,1)S(1)} %get-tuple-element.51.low_ref, bf16[2048,128]{1,0:T(8,128)(2,1)S(1)} %get-tuple-element.52.high_ref, bf16[512,256]{1,0:T(8,128)(2,1)S(1)} %collective-permute-done.5.refs_1_.refs_0_, ...), custom_call_target="tpu_custom_call" | custom-call | flops 536870912 | bytes 4194304 | tf_op jit(solution)/shard_map/pick_values/pallas_call | solution.py:370
  24.3 0.5 %collective-permute-start.6 = (bf16[16,2048]{1,0:T(8,128)(2,1)S(1)}, bf16[16,2048]{1,0:T(8,128)(2,1)S(1)}, u32[]{:S(2)}, u32[]{:S(2)}) collective-permute-start(bf16[16,2048]{1,0:T(8,128)(2,1)S(1)} %pick_values.5), channel_id=1, source_target_pairs={{0,2},{1,3},{2,0},{3,1},{4,6},{5,7},{6,4},{7,5},{8,10},{9,11},{10,... | collective-permute-start | bytes 196616 | tf_op jit(solution)/shard_map/ppermute | solution.py:390
  24.8 1.5 %pick_values.3 = bf16[16,2048]{1,0:T(8,128)(2,1)S(1)} custom-call(bf16[2048,256]{1,0:T(8,128)(2,1)S(1)} %get-tuple-element.44.x_ref, bf16[2048,128]{1,0:T(8,128)(2,1)S(1)} %get-tuple-element.45.low_ref, bf16[2048,128]{1,0:T(8,128)(2,1)S(1)} %get-tuple-element.46.high_ref, bf16[512,256]{1,0:T(8,128)(2,1)S(1)} %pad_maximum_fusion.refs_0_, ...), custom_call_target="tpu_custom_call" | custom-call | flops 1073741824 | bytes 4194304 | tf_op jit(solution)/shard_map/pick_values/pallas_call | solution.py:370
  26.3 2.3 %collective-permute-done.6 = bf16[16,2048]{1,0:T(8,128)(2,1)S(1)} collective-permute-done((bf16[16,2048]{1,0:T(8,128)(2,1)S(1)}, bf16[16,2048]{1,0:T(8,128)(2,1)S(1)}, u32[]{:S(2)}, u32[]{:S(2)}) %collective-permute-start.6) | collective-permute-done | bytes 65568 | tf_op jit(solution)/shard_map/ppermute | solution.py:390
  28.6 0.6 %fusion = bf16[2048,16]{0,1:T(8,128)(2,1)} fusion(bf16[16,2048]{1,0:T(8,128)(2,1)S(1)} %collective-permute-done.6, bf16[16,2048]{1,0:T(8,128)(2,1)S(1)} %pick_values.3), kind=kLoop, calls=%fused_computation.2 | loop fusion | flops 131072 | bytes 196608 | tf_op jit(solution)/shard_map/transpose | solution.py:469
  (2 shorter events, 0.0 us)
Async XLA Ops:
  1.4 10.7 %copy-start = (bf16[1,1024,1024]{2,1,0:T(8,128)(2,1)S(1)}, bf16[1,1024,1024]{2,1,0:T(8,128)(2,1)}, u32[]{:S(2)}) copy-start(bf16[1,1024,1024]{2,1,0:T(8,128)(2,1)} %param.11) | copy-start | bytes 6291460
  4.8 12.9 %collective-permute-start.4 = (bf16[1056,128]{1,0:T(8,128)(2,1)S(1)}, bf16[1056,128]{1,0:T(8,128)(2,1)S(1)}, u32[]{:S(2)}, u32[]{:S(2)}) collective-permute-start(bf16[1056,128]{1,0:T(8,128)(2,1)S(1)} %get-tuple-element.40), channel_id=1, source_target_pairs={{0,2},{1,3},{2,0},{3,1},{4,6},{5,7},{6,4},{7,5},{8,10},{9,11},{10,... | collective-permute-start | bytes 811016 | tf_op jit(solution)/shard_map/ppermute | solution.py:390
  7.8 4.3 %collective-permute-start = (bf16[32,1024]{1,0:T(8,128)(2,1)S(1)}, bf16[32,1024]{1,0:T(8,128)(2,1)S(1)}, u32[]{:S(2)}, u32[]{:S(2)}) collective-permute-start(bf16[32,1024]{1,0:T(8,128)(2,1)S(1)} %get-tuple-element.30), channel_id=1, source_target_pairs={{0,16},{16,0},{1,17},{17,1},{2,18},{18,2},{3,19},{19,3},{4,20},{20... | collective-permute-start | bytes 196616 | tf_op jit(solution)/shard_map/ppermute | solution.py:390
  12.8 6.1 %collective-permute-start.3 = (bf16[128,256]{1,0:T(8,128)(2,1)S(1)}, bf16[128,256]{1,0:T(8,128)(2,1)S(1)}, u32[]{:S(2)}, u32[]{:S(2)}) collective-permute-start(bf16[128,256]{1,0:T(8,128)(2,1)S(1)} %cycle_coefs.1), channel_id=1, source_target_pairs={{0,12},{4,8},{8,4},{12,0},{1,13},{5,9},{9,5},{13,1},{2,14},{6,10},... | collective-permute-start | bytes 196616 | tf_op jit(solution)/shard_map/ppermute | solution.py:390
  16.4 5.2 %collective-permute-start.2 = (bf16[128,256]{1,0:T(8,128)(2,1)S(1)}, bf16[128,256]{1,0:T(8,128)(2,1)S(1)}, u32[]{:S(2)}, u32[]{:S(2)}) collective-permute-start(bf16[128,256]{1,0:T(8,128)(2,1)S(1)} %cycle_coefs.1), channel_id=1, source_target_pairs={{0,8},{4,12},{8,0},{12,4},{1,9},{5,13},{9,1},{13,5},{2,10},{6,14},... | collective-permute-start | bytes 196616 | tf_op jit(solution)/shard_map/ppermute | solution.py:390
  16.4 5.2 %collective-permute-start.1 = (bf16[128,256]{1,0:T(8,128)(2,1)S(1)}, bf16[128,256]{1,0:T(8,128)(2,1)S(1)}, u32[]{:S(2)}, u32[]{:S(2)}) collective-permute-start(bf16[128,256]{1,0:T(8,128)(2,1)S(1)} %cycle_coefs.1), channel_id=1, source_target_pairs={{0,4},{4,0},{8,12},{12,8},{1,5},{5,1},{9,13},{13,9},{2,6},{6,2},{1... | collective-permute-start | bytes 196616 | tf_op jit(solution)/shard_map/ppermute | solution.py:390
  21.7 1.6 %collective-permute-start.5 = (bf16[512,256]{1,0:T(8,128)(2,1)S(1)}, bf16[512,256]{1,0:T(8,128)(2,1)S(1)}, u32[]{:S(2)}, u32[]{:S(2)}) collective-permute-start(bf16[512,256]{1,0:T(8,128)(2,1)S(1)} %pad_maximum_fusion.refs_0_), channel_id=1, source_target_pairs={{0,1},{1,0},{2,3},{3,2},{4,5},{5,4},{6,7},{7,6},{8,9},{9,8},{10,11... | collective-permute-start | bytes 786440 | tf_op jit(solution)/shard_map/ppermute | solution.py:390
  24.3 4.3 %collective-permute-start.6 = (bf16[16,2048]{1,0:T(8,128)(2,1)S(1)}, bf16[16,2048]{1,0:T(8,128)(2,1)S(1)}, u32[]{:S(2)}, u32[]{:S(2)}) collective-permute-start(bf16[16,2048]{1,0:T(8,128)(2,1)S(1)} %pick_values.5), channel_id=1, source_target_pairs={{0,2},{1,3},{2,0},{3,1},{4,6},{5,7},{6,4},{7,5},{8,10},{9,11},{10,... | collective-permute-start | bytes 196616 | tf_op jit(solution)/shard_map/ppermute | solution.py:390

commit v2 on v1

--- a/solution.py
+++ b/solution.py
@@ -111,6 +111,9 @@
         ],
         compiler_params=pltpu.CompilerParams(vmem_limit_bytes=SMALL),
         name="band_sums",
+        cost_estimate=pl.CostEstimate(
+            flops=2**31, bytes_accessed=2**23, transcendentals=0
+        ),
     )(*[in_hbm(value) for value in operands])
 
 
@@ -163,19 +166,11 @@
 
 
 def spread_kernel(
-    lanes_ref, code_ref, interp_hbm, near_ref, far_ref, base_ref, turn_ref, interp_ref, sem
+    lanes_ref, code_ref, interp_ref, near_ref, far_ref, base_ref, turn_ref
 ):
     samples, _ = interp_ref.shape
     lon_tiles = NPHI // TPHI
     rows = min(512, samples)
-    copies = []
-    for step in range(samples // rows):
-        here = pl.ds(step * rows, rows)
-        copies.append(
-            pltpu.make_async_copy(interp_hbm.at[here, :], interp_ref.at[here, :], sem.at[step])
-        )
-        copies[-1].start()
-
     place = iota((TPHI, 2 * LANES), 0)
     lane = iota((TPHI, 2 * LANES), 1)
     side = lane // LANES
@@ -215,7 +210,6 @@
         columns = jnp.concatenate([column_of(lon_tile[g : g + 1, :]) for g in groups])
         tile_hit = jnp.where(columns == tile_of_lane, 1.0, 0.0).astype(BF16)
         turn = jnp.dot(tile_hit, turn_ref[...], preferred_element_type=F32)
-        copies[step].wait()
         here = slice(step * rows, (step + 1) * rows)
         pair = jnp.dot(interp_ref[here, :], base_ref[...], preferred_element_type=F32) * turn
         both = pair[:, :LANES] + pair[:, LANES:]
@@ -238,12 +232,10 @@
         spread_kernel,
         out_shape=(packet, packet),
         in_specs=[pl.BlockSpec(memory_space=pltpu.VMEM)] * 2
-        + [pl.BlockSpec(memory_space=pltpu.HBM)],
+        + [pl.BlockSpec(memory_space=pltpu.VMEM)],
         scratch_shapes=[
             pltpu.VMEM((pixels, 2 * LANES), BF16),
             pltpu.VMEM((LANES, 2 * LANES), BF16),
-            pltpu.VMEM((samples, pixels), BF16),
-            pltpu.SemaphoreType.DMA((samples // min(512, samples),)),
         ],
         compiler_params=pltpu.CompilerParams(vmem_limit_bytes=SMALL),
         name="spread_samples",
@@ -252,7 +244,7 @@
             bytes_accessed=samples * pixels * 4,
             transcendentals=0,
         ),
-    )(order_lanes, code, in_hbm(interp))
+    )(order_lanes, code, interp)
 
 
 def unpack_kernel(packet_ref, x_ref, low_ref, high_ref):

time: 29.5 us -> 27.9 us (0.946)
  Pallas kernels: 9.69 us -> 8.07 us
    pallas_call x1, Pallas kernels: 3.32 us -> 1.51 us  [spread_samples(): pl.pallas_call(spread_kernel, out_shape=(packet, packet), in_specs=[pl.Bl...]
  transfers between devices with their start and end apart: 7 -> 7, of which waited for: 5 -> 5; matrix products, arithmetic and copies ran while one was open for 0% -> 0% of each run, Pallas kernels for 13% -> 14%
where the time goes in v2:
time: 27.9 us; the launch traced here: 27.8 us
  starting transfers between devices  9.56 us (34%)
  waiting for transfers between devices  9.19 us (33%)
  Pallas kernels  8.07 us (29%)
  other arithmetic  0.67 us (2%)
    ppermute x7, starting transfers between devices, swap(): return lax.ppermute(value, axis, [(i, i ^ step) for i in range(size)])  9.56 us
    ppermute x7, waiting for transfers between devices, swap(): return lax.ppermute(value, axis, [(i, i ^ step) for i in range(size)])  9.19 us
    pallas_call x3, Pallas kernels, pick_values(): pl.pallas_call(functools.partial(pick_kernel, counts, first * 2 * FOLD *...  3.32 us
    pallas_call x1, Pallas kernels, band_sums(): pl.pallas_call(functools.partial(band_kernel, tiles_each, slots), out_sha...  1.58 us
    pallas_call x1, Pallas kernels, spread_samples(): pl.pallas_call(spread_kernel, out_shape=(packet, packet), in_specs=[pl.Bl...  1.51 us
    pallas_call x2, Pallas kernels, unpack_samples(): pl.pallas_call(unpack_kernel, out_shape=(jax.ShapeDtypeStruct((samples, F...  1.02 us
    transpose x1, other arithmetic, on_device(): return (values.astype(F32) + other.astype(F32)).astype(BF16).T  0.65 us
    pallas_call x1, Pallas kernels, cycle_coefs(): pl.pallas_call(cycle_kernel, out_shape=jax.ShapeDtypeStruct((LANES, rows...  0.64 us
  transfers between devices with their start and end apart: 7, of which 5 were waited for; matrix products, arithmetic and copies ran while one was open for 0% of the time, Pallas kernels for 14%

profile of v2, /device:TPU:0, one launch (start us, length us, event | category | flops | bytes accessed | tf_op | source)
XLA Modules:
  0.0 27.8 jit_solution(14752089899879654668)
XLA Ops:
  0.0 1.6 %band_sums.1 = (f32[32,1024]{1,0:T(8,128)S(1)}, bf16[32,1024]{1,0:T(8,128)(2,1)S(1)}, s32[8,256]{1,0:T(8,128)S(1)}, s32[16,128]{1,0:T(8,128)S(1)}) custom-call(s32[32,32]{1,0:T(8,128)} %index_ref.1, f32[32,32]{1,0:T(8,128)} %weight_ref.1, s32[16]{0:T(128)} %orders_ref.1, s32[16,128]{1,0:T(8,128)} %bitcast.8, s32[16,128]{1,0:T(8,128)} %bitcast.9, ...), custom_call_target="tpu_custom_call" | custom-call | flops 2147483648 | bytes 8388608 | tf_op jit(solution)/shard_map/band_sums/pallas_call | solution.py:94
  1.6 0.2 copy-done.1
  1.8 1.5 %spread_samples.1 = (bf16[1056,128]{1,0:T(8,128)(2,1)S(1)}, bf16[1056,128]{1,0:T(8,128)(2,1)S(1)}) custom-call(s32[8,256]{1,0:T(8,128)S(1)} %get-tuple-element.31.lanes_ref, s32[16,128]{1,0:T(8,128)S(1)} %get-tuple-element.32.code_ref, bf16[2048,512]{1,0:T(8,128)(2,1)S(1)} %copy-done.1), custom_call_target="tpu_custom_call" | custom-call | flops 2147483648 | bytes 4194304 | tf_op jit(solution)/shard_map/spread_samples/pallas_call | solution.py:231
  3.3 3.1 %collective-permute-start.4 = (bf16[1056,128]{1,0:T(8,128)(2,1)S(1)}, bf16[1056,128]{1,0:T(8,128)(2,1)S(1)}, u32[]{:S(2)}, u32[]{:S(2)}) collective-permute-start(bf16[1056,128]{1,0:T(8,128)(2,1)S(1)} %get-tuple-element.40), channel_id=1, source_target_pairs={{0,2},{1,3},{2,0},{3,1},{4,6},{5,7},{6,4},{7,5},{8,10},{9,11},{10,... | collective-permute-start | bytes 811016 | tf_op jit(solution)/shard_map/ppermute | solution.py:382
  6.4 1.5 %collective-permute-start = (bf16[32,1024]{1,0:T(8,128)(2,1)S(1)}, bf16[32,1024]{1,0:T(8,128)(2,1)S(1)}, u32[]{:S(2)}, u32[]{:S(2)}) collective-permute-start(bf16[32,1024]{1,0:T(8,128)(2,1)S(1)} %get-tuple-element.30), channel_id=1, source_target_pairs={{0,16},{16,0},{1,17},{17,1},{2,18},{18,2},{3,19},{19,3},{4,20},{20... | collective-permute-start | bytes 196616 | tf_op jit(solution)/shard_map/ppermute | solution.py:382
  7.9 2.8 %collective-permute-done.recv_ref = bf16[32,1024]{1,0:T(8,128)(2,1)S(1)} collective-permute-done((bf16[32,1024]{1,0:T(8,128)(2,1)S(1)}, bf16[32,1024]{1,0:T(8,128)(2,1)S(1)}, u32[]{:S(2)}, u32[]{:S(2)}) %collective-permute-start) | collective-permute-done | bytes 65568 | tf_op jit(solution)/shard_map/ppermute | solution.py:382
  10.7 0.6 %cycle_coefs.1 = bf16[128,256]{1,0:T(8,128)(2,1)S(1)} custom-call(f32[32,1024]{1,0:T(8,128)S(1)} %get-tuple-element.29.own_ref, bf16[32,1024]{1,0:T(8,128)(2,1)S(1)} %collective-permute-done.recv_ref, bf16[1024,1024]{1,0:T(8,128)(2,1)S(1)} %bitcast.6), custom_call_target="tpu_custom_call" | custom-call | tf_op jit(solution)/shard_map/cycle_coefs/pallas_call | solution.py:142
  11.3 3.7 %collective-permute-start.3 = (bf16[128,256]{1,0:T(8,128)(2,1)S(1)}, bf16[128,256]{1,0:T(8,128)(2,1)S(1)}, u32[]{:S(2)}, u32[]{:S(2)}) collective-permute-start(bf16[128,256]{1,0:T(8,128)(2,1)S(1)} %cycle_coefs.1), channel_id=1, source_target_pairs={{0,12},{4,8},{8,4},{12,0},{1,13},{5,9},{9,5},{13,1},{2,14},{6,10},... | collective-permute-start | bytes 196616 | tf_op jit(solution)/shard_map/ppermute | solution.py:382
  15.0 0.0 collective-permute-start.2
  15.0 0.8 %collective-permute-start.1 = (bf16[128,256]{1,0:T(8,128)(2,1)S(1)}, bf16[128,256]{1,0:T(8,128)(2,1)S(1)}, u32[]{:S(2)}, u32[]{:S(2)}) collective-permute-start(bf16[128,256]{1,0:T(8,128)(2,1)S(1)} %cycle_coefs.1), channel_id=1, source_target_pairs={{0,4},{4,0},{8,12},{12,8},{1,5},{5,1},{9,13},{13,9},{2,6},{6,2},{1... | collective-permute-start | bytes 196616 | tf_op jit(solution)/shard_map/ppermute | solution.py:382
  15.8 0.5 %unpack_samples.2 = (bf16[2048,256]{1,0:T(8,128)(2,1)S(1)}, bf16[2048,128]{1,0:T(8,128)(2,1)S(1)}, bf16[2048,128]{1,0:T(8,128)(2,1)S(1)}) custom-call(bf16[1056,128]{1,0:T(8,128)(2,1)S(1)} %get-tuple-element.36.packet_ref), custom_call_target="tpu_custom_call" | custom-call | flops 268435456 | bytes 2097152 | tf_op jit(solution)/shard_map/unpack_samples/pallas_call | solution.py:271
  16.3 0.0 collective-permute-done.4.packet_ref
  16.3 0.5 %unpack_samples.3 = (bf16[2048,256]{1,0:T(8,128)(2,1)S(1)}, bf16[2048,128]{1,0:T(8,128)(2,1)S(1)}, bf16[2048,128]{1,0:T(8,128)(2,1)S(1)}) custom-call(bf16[1056,128]{1,0:T(8,128)(2,1)S(1)} %collective-permute-done.4.packet_ref), custom_call_target="tpu_custom_call" | custom-call | flops 268435456 | bytes 2097152 | tf_op jit(solution)/shard_map/unpack_samples/pallas_call | solution.py:271
  16.8 0.6 %collective-permute-done.3 = bf16[128,256]{1,0:T(8,128)(2,1)S(1)} collective-permute-done((bf16[128,256]{1,0:T(8,128)(2,1)S(1)}, bf16[128,256]{1,0:T(8,128)(2,1)S(1)}, u32[]{:S(2)}, u32[]{:S(2)}) %collective-permute-start.3) | collective-permute-done | bytes 65568 | tf_op jit(solution)/shard_map/ppermute | solution.py:382
  17.4 2.7 %collective-permute-done.2 = bf16[128,256]{1,0:T(8,128)(2,1)S(1)} collective-permute-done((bf16[128,256]{1,0:T(8,128)(2,1)S(1)}, bf16[128,256]{1,0:T(8,128)(2,1)S(1)}, u32[]{:S(2)}, u32[]{:S(2)}) %collective-permute-start.2) | collective-permute-done | bytes 65568 | tf_op jit(solution)/shard_map/ppermute | solution.py:382
  20.2 0.0 collective-permute-done.1
  20.2 0.1 collective-permute-start.5
  20.3 0.7 %pick_values.4.refs_1_ = f32[2048,256]{1,0:T(8,128)S(1)} custom-call(bf16[2048,256]{1,0:T(8,128)(2,1)S(1)} %get-tuple-element.50.x_ref, bf16[2048,128]{1,0:T(8,128)(2,1)S(1)} %get-tuple-element.51.low_ref, bf16[2048,128]{1,0:T(8,128)(2,1)S(1)} %get-tuple-element.52.high_ref, bf16[512,256]{1,0:T(8,128)(2,1)S(1)} %pad_maximum_fusion.refs_0_), custom_call_target="tpu_custom_call" | custom-call | flops 536870912 | bytes 4194304 | tf_op jit(solution)/shard_map/pick_values/pallas_call | solution.py:362
  21.0 0.8 %collective-permute-done.5.refs_1_.refs_0_ = bf16[512,256]{1,0:T(8,128)(2,1)S(1)} collective-permute-done((bf16[512,256]{1,0:T(8,128)(2,1)S(1)}, bf16[512,256]{1,0:T(8,128)(2,1)S(1)}, u32[]{:S(2)}, u32[]{:S(2)}) %collective-permute-start.5) | collective-permute-done | bytes 262176 | tf_op jit(solution)/shard_map/ppermute | solution.py:382
  21.8 1.0 %pick_values.5 = bf16[16,2048]{1,0:T(8,128)(2,1)S(1)} custom-call(bf16[2048,256]{1,0:T(8,128)(2,1)S(1)} %get-tuple-element.50.x_ref, bf16[2048,128]{1,0:T(8,128)(2,1)S(1)} %get-tuple-element.51.low_ref, bf16[2048,128]{1,0:T(8,128)(2,1)S(1)} %get-tuple-element.52.high_ref, bf16[512,256]{1,0:T(8,128)(2,1)S(1)} %collective-permute-done.5.refs_1_.refs_0_, ...), custom_call_target="tpu_custom_call" | custom-call | flops 536870912 | bytes 4194304 | tf_op jit(solution)/shard_map/pick_values/pallas_call | solution.py:362
  22.8 0.5 %collective-permute-start.6 = (bf16[16,2048]{1,0:T(8,128)(2,1)S(1)}, bf16[16,2048]{1,0:T(8,128)(2,1)S(1)}, u32[]{:S(2)}, u32[]{:S(2)}) collective-permute-start(bf16[16,2048]{1,0:T(8,128)(2,1)S(1)} %pick_values.5), channel_id=1, source_target_pairs={{0,2},{1,3},{2,0},{3,1},{4,6},{5,7},{6,4},{7,5},{8,10},{9,11},{10,... | collective-permute-start | bytes 196616 | tf_op jit(solution)/shard_map/ppermute | solution.py:382
  23.3 1.6 %pick_values.3 = bf16[16,2048]{1,0:T(8,128)(2,1)S(1)} custom-call(bf16[2048,256]{1,0:T(8,128)(2,1)S(1)} %get-tuple-element.44.x_ref, bf16[2048,128]{1,0:T(8,128)(2,1)S(1)} %get-tuple-element.45.low_ref, bf16[2048,128]{1,0:T(8,128)(2,1)S(1)} %get-tuple-element.46.high_ref, bf16[512,256]{1,0:T(8,128)(2,1)S(1)} %pad_maximum_fusion.refs_0_, ...), custom_call_target="tpu_custom_call" | custom-call | flops 1073741824 | bytes 4194304 | tf_op jit(solution)/shard_map/pick_values/pallas_call | solution.py:362
  24.9 2.2 %collective-permute-done.6 = bf16[16,2048]{1,0:T(8,128)(2,1)S(1)} collective-permute-done((bf16[16,2048]{1,0:T(8,128)(2,1)S(1)}, bf16[16,2048]{1,0:T(8,128)(2,1)S(1)}, u32[]{:S(2)}, u32[]{:S(2)}) %collective-permute-start.6) | collective-permute-done | bytes 65568 | tf_op jit(solution)/shard_map/ppermute | solution.py:382
  27.1 0.6 %fusion = bf16[2048,16]{0,1:T(8,128)(2,1)} fusion(bf16[16,2048]{1,0:T(8,128)(2,1)S(1)} %collective-permute-done.6, bf16[16,2048]{1,0:T(8,128)(2,1)S(1)} %pick_values.3), kind=kLoop, calls=%fused_computation.2 | loop fusion | flops 131072 | bytes 196608 | tf_op jit(solution)/shard_map/transpose | solution.py:461
  (4 shorter events, 0.0 us)
Async XLA Ops:
  0.0 1.8 %copy-start.1 = (bf16[2048,512]{1,0:T(8,128)(2,1)S(1)}, bf16[2048,512]{1,0:T(8,128)(2,1)}, u32[]{:S(2)}) copy-start(bf16[2048,512]{1,0:T(8,128)(2,1)} %interp_ref.1) | copy-start | bytes 6291460
  1.8 8.8 %copy-start = (bf16[1,1024,1024]{2,1,0:T(8,128)(2,1)S(1)}, bf16[1,1024,1024]{2,1,0:T(8,128)(2,1)}, u32[]{:S(2)}) copy-start(bf16[1,1024,1024]{2,1,0:T(8,128)(2,1)} %param.11) | copy-start | bytes 6291460
  3.3 12.9 %collective-permute-start.4 = (bf16[1056,128]{1,0:T(8,128)(2,1)S(1)}, bf16[1056,128]{1,0:T(8,128)(2,1)S(1)}, u32[]{:S(2)}, u32[]{:S(2)}) collective-permute-start(bf16[1056,128]{1,0:T(8,128)(2,1)S(1)} %get-tuple-element.40), channel_id=1, source_target_pairs={{0,2},{1,3},{2,0},{3,1},{4,6},{5,7},{6,4},{7,5},{8,10},{9,11},{10,... | collective-permute-start | bytes 811016 | tf_op jit(solution)/shard_map/ppermute | solution.py:382
  6.4 4.3 %collective-permute-start = (bf16[32,1024]{1,0:T(8,128)(2,1)S(1)}, bf16[32,1024]{1,0:T(8,128)(2,1)S(1)}, u32[]{:S(2)}, u32[]{:S(2)}) collective-permute-start(bf16[32,1024]{1,0:T(8,128)(2,1)S(1)} %get-tuple-element.30), channel_id=1, source_target_pairs={{0,16},{16,0},{1,17},{17,1},{2,18},{18,2},{3,19},{19,3},{4,20},{20... | collective-permute-start | bytes 196616 | tf_op jit(solution)/shard_map/ppermute | solution.py:382
  11.3 6.1 %collective-permute-start.3 = (bf16[128,256]{1,0:T(8,128)(2,1)S(1)}, bf16[128,256]{1,0:T(8,128)(2,1)S(1)}, u32[]{:S(2)}, u32[]{:S(2)}) collective-permute-start(bf16[128,256]{1,0:T(8,128)(2,1)S(1)} %cycle_coefs.1), channel_id=1, source_target_pairs={{0,12},{4,8},{8,4},{12,0},{1,13},{5,9},{9,5},{13,1},{2,14},{6,10},... | collective-permute-start | bytes 196616 | tf_op jit(solution)/shard_map/ppermute | solution.py:382
  15.0 5.2 %collective-permute-start.2 = (bf16[128,256]{1,0:T(8,128)(2,1)S(1)}, bf16[128,256]{1,0:T(8,128)(2,1)S(1)}, u32[]{:S(2)}, u32[]{:S(2)}) collective-permute-start(bf16[128,256]{1,0:T(8,128)(2,1)S(1)} %cycle_coefs.1), channel_id=1, source_target_pairs={{0,8},{4,12},{8,0},{12,4},{1,9},{5,13},{9,1},{13,5},{2,10},{6,14},... | collective-permute-start | bytes 196616 | tf_op jit(solution)/shard_map/ppermute | solution.py:382
  15.0 5.2 %collective-permute-start.1 = (bf16[128,256]{1,0:T(8,128)(2,1)S(1)}, bf16[128,256]{1,0:T(8,128)(2,1)S(1)}, u32[]{:S(2)}, u32[]{:S(2)}) collective-permute-start(bf16[128,256]{1,0:T(8,128)(2,1)S(1)} %cycle_coefs.1), channel_id=1, source_target_pairs={{0,4},{4,0},{8,12},{12,8},{1,5},{5,1},{9,13},{13,9},{2,6},{6,2},{1... | collective-permute-start | bytes 196616 | tf_op jit(solution)/shard_map/ppermute | solution.py:382
  20.2 1.6 %collective-permute-start.5 = (bf16[512,256]{1,0:T(8,128)(2,1)S(1)}, bf16[512,256]{1,0:T(8,128)(2,1)S(1)}, u32[]{:S(2)}, u32[]{:S(2)}) collective-permute-start(bf16[512,256]{1,0:T(8,128)(2,1)S(1)} %pad_maximum_fusion.refs_0_), channel_id=1, source_target_pairs={{0,1},{1,0},{2,3},{3,2},{4,5},{5,4},{6,7},{7,6},{8,9},{9,8},{10,11... | collective-permute-start | bytes 786440 | tf_op jit(solution)/shard_map/ppermute | solution.py:382
  22.8 4.3 %collective-permute-start.6 = (bf16[16,2048]{1,0:T(8,128)(2,1)S(1)}, bf16[16,2048]{1,0:T(8,128)(2,1)S(1)}, u32[]{:S(2)}, u32[]{:S(2)}) collective-permute-start(bf16[16,2048]{1,0:T(8,128)(2,1)S(1)} %pick_values.5), channel_id=1, source_target_pairs={{0,2},{1,3},{2,0},{3,1},{4,6},{5,7},{6,4},{7,5},{8,10},{9,11},{10,... | collective-permute-start | bytes 196616 | tf_op jit(solution)/shard_map/ppermute | solution.py:382

commit v3 on v2

--- a/solution.py
+++ b/solution.py
@@ -447,17 +447,24 @@
     got = swap(far_packet, "sub", far)
     received, near_packet = lax.optimization_barrier((received, near_packet))
     piece = cycle_coefs(own, received, legendre[0])
-    gathered = [swap(piece, "grp", g) for g in range(1, group_count)]
+    gathered = []
+    for g in range(1, group_count):
+        gathered.append(swap(piece, "grp", g))
     near_packet, _ = lax.optimization_barrier((near_packet, piece))
     near_x = unpack_samples(near_packet, samples)
     far_x = unpack_samples(got, samples)
-    gathered, near_x, far_x = lax.optimization_barrier((gathered, near_x, far_x))
-    stack = jnp.concatenate([piece] + gathered)
-    stacks = [stack] + [swap(stack, "sub", s) for s in range(1, far)]
-    sums = pick_values(*far_x, stacks[:1], 0, None, None)
-    far_values = pick_values(*far_x, stacks[1:], group_count, sums, dets)
+    gathered[1], near_x, far_x = lax.optimization_barrier(
+        (gathered[1], near_x, far_x)
+    )
+    pieces = [piece] + gathered
+    others = []
+    for s in range(1, far):
+        for held in pieces:
+            others.append(swap(held, "sub", s))
+    sums = pick_values(*far_x, pieces, 0, None, None)
+    far_values = pick_values(*far_x, others, group_count, sums, dets)
     other = swap(far_values, "sub", far)
-    values = pick_values(*near_x, stacks, 0, None, dets)
+    values = pick_values(*near_x, pieces + others, 0, None, dets)
     return (values.astype(F32) + other.astype(F32)).astype(BF16).T
 
 

time: 27.9 us -> 28.7 us (1.029)
  waiting for transfers between devices: 9.19 us -> 9.65 us
  starting transfers between devices: 9.56 us -> 9.89 us
    ppermute x7 -> x10, waiting for transfers between devices: 9.19 us -> 9.65 us  [swap(): return lax.ppermute(value, axis, [(i, i ^ step) for i in range(size)])]
    ppermute x7 -> x10, starting transfers between devices: 9.56 us -> 9.89 us  [swap(): return lax.ppermute(value, axis, [(i, i ^ step) for i in range(size)])]
  transfers between devices with their start and end apart: 7 -> 10, of which waited for: 5 -> 5; matrix products, arithmetic and copies ran while one was open for 0% -> 0% of each run, Pallas kernels for 14% -> 14%
where the time goes in v3:
time: 28.7 us; the launch traced here: 28.5 us
  starting transfers between devices  9.89 us (34%)
  waiting for transfers between devices  9.65 us (34%)
  Pallas kernels  8.03 us (28%)
  other arithmetic  0.65 us (2%)
    ppermute x10, starting transfers between devices, swap(): return lax.ppermute(value, axis, [(i, i ^ step) for i in range(size)])  9.89 us
    ppermute x10, waiting for transfers between devices, swap(): return lax.ppermute(value, axis, [(i, i ^ step) for i in range(size)])  9.65 us
    pallas_call x3, Pallas kernels, pick_values(): pl.pallas_call(functools.partial(pick_kernel, counts, first * 2 * FOLD *...  3.27 us
    pallas_call x1, Pallas kernels, band_sums(): pl.pallas_call(functools.partial(band_kernel, tiles_each, slots), out_sha...  1.58 us
    pallas_call x1, Pallas kernels, spread_samples(): pl.pallas_call(spread_kernel, out_shape=(packet, packet), in_specs=[pl.Bl...  1.51 us
    pallas_call x2, Pallas kernels, unpack_samples(): pl.pallas_call(unpack_kernel, out_shape=(jax.ShapeDtypeStruct((samples, F...  1.03 us
    transpose x1, other arithmetic, on_device(): return (values.astype(F32) + other.astype(F32)).astype(BF16).T  0.65 us
    pallas_call x1, Pallas kernels, cycle_coefs(): pl.pallas_call(cycle_kernel, out_shape=jax.ShapeDtypeStruct((LANES, rows...  0.64 us
  transfers between devices with their start and end apart: 10, of which 5 were waited for; matrix products, arithmetic and copies ran while one was open for 0% of the time, Pallas kernels for 14%

profile of v3, /device:TPU:0, one launch (start us, length us, event | category | flops | bytes accessed | tf_op | source)
XLA Modules:
  0.0 28.5 jit_solution(9985924698636925923)
XLA Ops:
  0.0 1.6 %band_sums.1 = (f32[32,1024]{1,0:T(8,128)S(1)}, bf16[32,1024]{1,0:T(8,128)(2,1)S(1)}, s32[8,256]{1,0:T(8,128)S(1)}, s32[16,128]{1,0:T(8,128)S(1)}) custom-call(s32[32,32]{1,0:T(8,128)} %index_ref.1, f32[32,32]{1,0:T(8,128)} %weight_ref.1, s32[16]{0:T(128)} %orders_ref.1, s32[16,128]{1,0:T(8,128)} %bitcast.8, s32[16,128]{1,0:T(8,128)} %bitcast.9, ...), custom_call_target="tpu_custom_call" | custom-call | flops 2147483648 | bytes 8388608 | tf_op jit(solution)/shard_map/band_sums/pallas_call | solution.py:94
  1.6 0.2 copy-done.1
  1.8 1.5 %spread_samples.1 = (bf16[1056,128]{1,0:T(8,128)(2,1)S(1)}, bf16[1056,128]{1,0:T(8,128)(2,1)S(1)}) custom-call(s32[8,256]{1,0:T(8,128)S(1)} %get-tuple-element.29.lanes_ref, s32[16,128]{1,0:T(8,128)S(1)} %get-tuple-element.30.code_ref, bf16[2048,512]{1,0:T(8,128)(2,1)S(1)} %copy-done.1), custom_call_target="tpu_custom_call" | custom-call | flops 2147483648 | bytes 4194304 | tf_op jit(solution)/shard_map/spread_samples/pallas_call | solution.py:231
  3.3 3.1 %collective-permute-start.2 = (bf16[1056,128]{1,0:T(8,128)(2,1)S(1)}, bf16[1056,128]{1,0:T(8,128)(2,1)S(1)}, u32[]{:S(2)}, u32[]{:S(2)}) collective-permute-start(bf16[1056,128]{1,0:T(8,128)(2,1)S(1)} %get-tuple-element.38), channel_id=1, source_target_pairs={{0,2},{1,3},{2,0},{3,1},{4,6},{5,7},{6,4},{7,5},{8,10},{9,11},{10,... | collective-permute-start | bytes 811016 | tf_op jit(solution)/shard_map/ppermute | solution.py:382
  6.4 1.5 %collective-permute-start = (bf16[32,1024]{1,0:T(8,128)(2,1)S(1)}, bf16[32,1024]{1,0:T(8,128)(2,1)S(1)}, u32[]{:S(2)}, u32[]{:S(2)}) collective-permute-start(bf16[32,1024]{1,0:T(8,128)(2,1)S(1)} %get-tuple-element.28), channel_id=1, source_target_pairs={{0,16},{16,0},{1,17},{17,1},{2,18},{18,2},{3,19},{19,3},{4,20},{20... | collective-permute-start | bytes 196616 | tf_op jit(solution)/shard_map/ppermute | solution.py:382
  7.9 2.8 %collective-permute-done.recv_ref = bf16[32,1024]{1,0:T(8,128)(2,1)S(1)} collective-permute-done((bf16[32,1024]{1,0:T(8,128)(2,1)S(1)}, bf16[32,1024]{1,0:T(8,128)(2,1)S(1)}, u32[]{:S(2)}, u32[]{:S(2)}) %collective-permute-start) | collective-permute-done | bytes 65568 | tf_op jit(solution)/shard_map/ppermute | solution.py:382
  10.7 0.6 %cycle_coefs.1.refs_0_ = bf16[128,256]{1,0:T(8,128)(2,1)S(1)} custom-call(f32[32,1024]{1,0:T(8,128)S(1)} %get-tuple-element.27.own_ref, bf16[32,1024]{1,0:T(8,128)(2,1)S(1)} %collective-permute-done.recv_ref, bf16[1024,1024]{1,0:T(8,128)(2,1)S(1)} %bitcast.6), custom_call_target="tpu_custom_call" | custom-call | tf_op jit(solution)/shard_map/cycle_coefs/pallas_call | solution.py:142
  11.3 1.6 %collective-permute-start.3 = (bf16[128,256]{1,0:T(8,128)(2,1)S(1)}, bf16[128,256]{1,0:T(8,128)(2,1)S(1)}, u32[]{:S(2)}, u32[]{:S(2)}) collective-permute-start(bf16[128,256]{1,0:T(8,128)(2,1)S(1)} %cycle_coefs.1.refs_0_), channel_id=1, source_target_pairs={{0,4},{4,0},{8,12},{12,8},{1,5},{5,1},{9,13},{13,9},{2,6},{6,2},{1... | collective-permute-start | bytes 196616 | tf_op jit(solution)/shard_map/ppermute | solution.py:382
  12.9 2.5 %collective-permute-start.4 = (bf16[128,256]{1,0:T(8,128)(2,1)S(1)}, bf16[128,256]{1,0:T(8,128)(2,1)S(1)}, u32[]{:S(2)}, u32[]{:S(2)}) collective-permute-start(bf16[128,256]{1,0:T(8,128)(2,1)S(1)} %cycle_coefs.1.refs_0_), channel_id=1, source_target_pairs={{0,12},{4,8},{8,4},{12,0},{1,13},{5,9},{9,5},{13,1},{2,14},{6,10},... | collective-permute-start | bytes 196616 | tf_op jit(solution)/shard_map/ppermute | solution.py:382
  15.4 0.1 collective-permute-start.1
  15.5 0.0 collective-permute-start.5
  15.5 0.5 %unpack_samples.2 = (bf16[2048,256]{1,0:T(8,128)(2,1)S(1)}, bf16[2048,128]{1,0:T(8,128)(2,1)S(1)}, bf16[2048,128]{1,0:T(8,128)(2,1)S(1)}) custom-call(bf16[1056,128]{1,0:T(8,128)(2,1)S(1)} %get-tuple-element.34.packet_ref), custom_call_target="tpu_custom_call" | custom-call | flops 268435456 | bytes 2097152 | tf_op jit(solution)/shard_map/unpack_samples/pallas_call | solution.py:271
  16.1 0.0 collective-permute-done.3.refs_1_
  16.1 0.6 %collective-permute-start.6 = (bf16[128,256]{1,0:T(8,128)(2,1)S(1)}, bf16[128,256]{1,0:T(8,128)(2,1)S(1)}, u32[]{:S(2)}, u32[]{:S(2)}) collective-permute-start(bf16[128,256]{1,0:T(8,128)(2,1)S(1)} %collective-permute-done.3.refs_1_), channel_id=1, source_target_pairs={{0,1},{1,0},{2,3},{3,2},{4,5},{5,4},{6,7},{7,6},{8,9},{9,8},{10,11... | collective-permute-start | bytes 196616 | tf_op jit(solution)/shard_map/ppermute | solution.py:382
  16.7 2.5 %collective-permute-done.4.refs_3_ = bf16[128,256]{1,0:T(8,128)(2,1)S(1)} collective-permute-done((bf16[128,256]{1,0:T(8,128)(2,1)S(1)}, bf16[128,256]{1,0:T(8,128)(2,1)S(1)}, u32[]{:S(2)}, u32[]{:S(2)}) %collective-permute-start.4) | collective-permute-done | bytes 65568 | tf_op jit(solution)/shard_map/ppermute | solution.py:382
  19.2 0.5 %unpack_samples.3 = (bf16[2048,256]{1,0:T(8,128)(2,1)S(1)}, bf16[2048,128]{1,0:T(8,128)(2,1)S(1)}, bf16[2048,128]{1,0:T(8,128)(2,1)S(1)}) custom-call(bf16[1056,128]{1,0:T(8,128)(2,1)S(1)} %collective-permute-done.2.packet_ref), custom_call_target="tpu_custom_call" | custom-call | flops 268435456 | bytes 2097152 | tf_op jit(solution)/shard_map/unpack_samples/pallas_call | solution.py:271
  19.7 1.6 %collective-permute-done.1.refs_2_ = bf16[128,256]{1,0:T(8,128)(2,1)S(1)} collective-permute-done((bf16[128,256]{1,0:T(8,128)(2,1)S(1)}, bf16[128,256]{1,0:T(8,128)(2,1)S(1)}, u32[]{:S(2)}, u32[]{:S(2)}) %collective-permute-start.1) | collective-permute-done | bytes 65568 | tf_op jit(solution)/shard_map/ppermute | solution.py:382
  21.3 0.7 %pick_values.4.refs_4_ = f32[2048,256]{1,0:T(8,128)S(1)} custom-call(bf16[2048,256]{1,0:T(8,128)(2,1)S(1)} %get-tuple-element.46.x_ref, bf16[2048,128]{1,0:T(8,128)(2,1)S(1)} %get-tuple-element.47.low_ref, bf16[2048,128]{1,0:T(8,128)(2,1)S(1)} %get-tuple-element.48.high_ref, bf16[128,256]{1,0:T(8,128)(2,1)S(1)} %cycle_coefs.1.refs_0_, ...), custom_call_target="tpu_custom_call" | custom-call | flops 536870912 | bytes 4194304 | tf_op jit(solution)/shard_map/pick_values/pallas_call | solution.py:362
  22.0 0.5 %collective-permute-done.7.refs_6_.refs_2_ = bf16[128,256]{1,0:T(8,128)(2,1)S(1)} collective-permute-done((bf16[128,256]{1,0:T(8,128)(2,1)S(1)}, bf16[128,256]{1,0:T(8,128)(2,1)S(1)}, u32[]{:S(2)}, u32[]{:S(2)}) %collective-permute-start.7) | collective-permute-done | bytes 65568 | tf_op jit(solution)/shard_map/ppermute | solution.py:382
  22.5 1.0 %pick_values.5 = bf16[16,2048]{1,0:T(8,128)(2,1)S(1)} custom-call(bf16[2048,256]{1,0:T(8,128)(2,1)S(1)} %get-tuple-element.46.x_ref, bf16[2048,128]{1,0:T(8,128)(2,1)S(1)} %get-tuple-element.47.low_ref, bf16[2048,128]{1,0:T(8,128)(2,1)S(1)} %get-tuple-element.48.high_ref, bf16[128,256]{1,0:T(8,128)(2,1)S(1)} %collective-permute-done.5.refs_4_.refs_0_, ...), custom_call_target="tpu_custom_call" | custom-call | flops 536870912 | bytes 4194304 | tf_op jit(solution)/shard_map/pick_values/pallas_call | solution.py:362
  23.6 0.5 %collective-permute-start.9 = (bf16[16,2048]{1,0:T(8,128)(2,1)S(1)}, bf16[16,2048]{1,0:T(8,128)(2,1)S(1)}, u32[]{:S(2)}, u32[]{:S(2)}) collective-permute-start(bf16[16,2048]{1,0:T(8,128)(2,1)S(1)} %pick_values.5), channel_id=1, source_target_pairs={{0,2},{1,3},{2,0},{3,1},{4,6},{5,7},{6,4},{7,5},{8,10},{9,11},{10,... | collective-permute-start | bytes 196616 | tf_op jit(solution)/shard_map/ppermute | solution.py:382
  24.1 1.5 %pick_values.3 = bf16[16,2048]{1,0:T(8,128)(2,1)S(1)} custom-call(bf16[2048,256]{1,0:T(8,128)(2,1)S(1)} %get-tuple-element.42.x_ref, bf16[2048,128]{1,0:T(8,128)(2,1)S(1)} %get-tuple-element.43.low_ref, bf16[2048,128]{1,0:T(8,128)(2,1)S(1)} %get-tuple-element.44.high_ref, bf16[128,256]{1,0:T(8,128)(2,1)S(1)} %cycle_coefs.1.refs_0_, ...), custom_call_target="tpu_custom_call" | custom-call | flops 1073741824 | bytes 4194304 | tf_op jit(solution)/shard_map/pick_values/pallas_call | solution.py:362
  25.6 2.3 %collective-permute-done.9 = bf16[16,2048]{1,0:T(8,128)(2,1)S(1)} collective-permute-done((bf16[16,2048]{1,0:T(8,128)(2,1)S(1)}, bf16[16,2048]{1,0:T(8,128)(2,1)S(1)}, u32[]{:S(2)}, u32[]{:S(2)}) %collective-permute-start.9) | collective-permute-done | bytes 65568 | tf_op jit(solution)/shard_map/ppermute | solution.py:382
  27.9 0.6 %fusion = bf16[2048,16]{0,1:T(8,128)(2,1)} fusion(bf16[16,2048]{1,0:T(8,128)(2,1)S(1)} %collective-permute-done.9, bf16[16,2048]{1,0:T(8,128)(2,1)S(1)} %pick_values.3), kind=kLoop, calls=%fused_computation.1 | loop fusion | flops 131072 | bytes 196608 | tf_op jit(solution)/shard_map/transpose | solution.py:468
  (9 shorter events, 0.0 us)
Async XLA Ops:
  0.0 1.8 %copy-start.1 = (bf16[2048,512]{1,0:T(8,128)(2,1)S(1)}, bf16[2048,512]{1,0:T(8,128)(2,1)}, u32[]{:S(2)}) copy-start(bf16[2048,512]{1,0:T(8,128)(2,1)} %interp_ref.1) | copy-start | bytes 6291460
  1.8 8.8 %copy-start = (bf16[1,1024,1024]{2,1,0:T(8,128)(2,1)S(1)}, bf16[1,1024,1024]{2,1,0:T(8,128)(2,1)}, u32[]{:S(2)}) copy-start(bf16[1,1024,1024]{2,1,0:T(8,128)(2,1)} %param.11) | copy-start | bytes 6291460
  3.3 15.8 %collective-permute-start.2 = (bf16[1056,128]{1,0:T(8,128)(2,1)S(1)}, bf16[1056,128]{1,0:T(8,128)(2,1)S(1)}, u32[]{:S(2)}, u32[]{:S(2)}) collective-permute-start(bf16[1056,128]{1,0:T(8,128)(2,1)S(1)} %get-tuple-element.38), channel_id=1, source_target_pairs={{0,2},{1,3},{2,0},{3,1},{4,6},{5,7},{6,4},{7,5},{8,10},{9,11},{10,... | collective-permute-start | bytes 811016 | tf_op jit(solution)/shard_map/ppermute | solution.py:382
  6.4 4.3 %collective-permute-start = (bf16[32,1024]{1,0:T(8,128)(2,1)S(1)}, bf16[32,1024]{1,0:T(8,128)(2,1)S(1)}, u32[]{:S(2)}, u32[]{:S(2)}) collective-permute-start(bf16[32,1024]{1,0:T(8,128)(2,1)S(1)} %get-tuple-element.28), channel_id=1, source_target_pairs={{0,16},{16,0},{1,17},{17,1},{2,18},{18,2},{3,19},{19,3},{4,20},{20... | collective-permute-start | bytes 196616 | tf_op jit(solution)/shard_map/ppermute | solution.py:382
  11.3 4.8 %collective-permute-start.3 = (bf16[128,256]{1,0:T(8,128)(2,1)S(1)}, bf16[128,256]{1,0:T(8,128)(2,1)S(1)}, u32[]{:S(2)}, u32[]{:S(2)}) collective-permute-start(bf16[128,256]{1,0:T(8,128)(2,1)S(1)} %cycle_coefs.1.refs_0_), channel_id=1, source_target_pairs={{0,4},{4,0},{8,12},{12,8},{1,5},{5,1},{9,13},{13,9},{2,6},{6,2},{1... | collective-permute-start | bytes 196616 | tf_op jit(solution)/shard_map/ppermute | solution.py:382
  12.9 6.2 %collective-permute-start.4 = (bf16[128,256]{1,0:T(8,128)(2,1)S(1)}, bf16[128,256]{1,0:T(8,128)(2,1)S(1)}, u32[]{:S(2)}, u32[]{:S(2)}) collective-permute-start(bf16[128,256]{1,0:T(8,128)(2,1)S(1)} %cycle_coefs.1.refs_0_), channel_id=1, source_target_pairs={{0,12},{4,8},{8,4},{12,0},{1,13},{5,9},{9,5},{13,1},{2,14},{6,10},... | collective-permute-start | bytes 196616 | tf_op jit(solution)/shard_map/ppermute | solution.py:382
  15.4 5.9 %collective-permute-start.1 = (bf16[128,256]{1,0:T(8,128)(2,1)S(1)}, bf16[128,256]{1,0:T(8,128)(2,1)S(1)}, u32[]{:S(2)}, u32[]{:S(2)}) collective-permute-start(bf16[128,256]{1,0:T(8,128)(2,1)S(1)} %cycle_coefs.1.refs_0_), channel_id=1, source_target_pairs={{0,8},{4,12},{8,0},{12,4},{1,9},{5,13},{9,1},{13,5},{2,10},{6,14},... | collective-permute-start | bytes 196616 | tf_op jit(solution)/shard_map/ppermute | solution.py:382
  15.5 6.5 %collective-permute-start.5 = (bf16[128,256]{1,0:T(8,128)(2,1)S(1)}, bf16[128,256]{1,0:T(8,128)(2,1)S(1)}, u32[]{:S(2)}, u32[]{:S(2)}) collective-permute-start(bf16[128,256]{1,0:T(8,128)(2,1)S(1)} %cycle_coefs.1.refs_0_), channel_id=1, source_target_pairs={{0,1},{1,0},{2,3},{3,2},{4,5},{5,4},{6,7},{7,6},{8,9},{9,8},{10,11... | collective-permute-start | bytes 196616 | tf_op jit(solution)/shard_map/ppermute | solution.py:382
  16.1 6.0 %collective-permute-start.6 = (bf16[128,256]{1,0:T(8,128)(2,1)S(1)}, bf16[128,256]{1,0:T(8,128)(2,1)S(1)}, u32[]{:S(2)}, u32[]{:S(2)}) collective-permute-start(bf16[128,256]{1,0:T(8,128)(2,1)S(1)} %collective-permute-done.3.refs_1_), channel_id=1, source_target_pairs={{0,1},{1,0},{2,3},{3,2},{4,5},{5,4},{6,7},{7,6},{8,9},{9,8},{10,11... | collective-permute-start | bytes 196616 | tf_op jit(solution)/shard_map/ppermute | solution.py:382
  19.2 2.9 %collective-permute-start.8 = (bf16[128,256]{1,0:T(8,128)(2,1)S(1)}, bf16[128,256]{1,0:T(8,128)(2,1)S(1)}, u32[]{:S(2)}, u32[]{:S(2)}) collective-permute-start(bf16[128,256]{1,0:T(8,128)(2,1)S(1)} %collective-permute-done.4.refs_3_), channel_id=1, source_target_pairs={{0,1},{1,0},{2,3},{3,2},{4,5},{5,4},{6,7},{7,6},{8,9},{9,8},{10,11... | collective-permute-start | bytes 196616 | tf_op jit(solution)/shard_map/ppermute | solution.py:382
  21.3 1.3 %collective-permute-start.7 = (bf16[128,256]{1,0:T(8,128)(2,1)S(1)}, bf16[128,256]{1,0:T(8,128)(2,1)S(1)}, u32[]{:S(2)}, u32[]{:S(2)}) collective-permute-start(bf16[128,256]{1,0:T(8,128)(2,1)S(1)} %collective-permute-done.1.refs_2_), channel_id=1, source_target_pairs={{0,1},{1,0},{2,3},{3,2},{4,5},{5,4},{6,7},{7,6},{8,9},{9,8},{10,11... | collective-permute-start | bytes 196616 | tf_op jit(solution)/shard_map/ppermute | solution.py:382
  23.6 4.3 %collective-permute-start.9 = (bf16[16,2048]{1,0:T(8,128)(2,1)S(1)}, bf16[16,2048]{1,0:T(8,128)(2,1)S(1)}, u32[]{:S(2)}, u32[]{:S(2)}) collective-permute-start(bf16[16,2048]{1,0:T(8,128)(2,1)S(1)} %pick_values.5), channel_id=1, source_target_pairs={{0,2},{1,3},{2,0},{3,1},{4,6},{5,7},{6,4},{7,5},{8,10},{9,11},{10,... | collective-permute-start | bytes 196616 | tf_op jit(solution)/shard_map/ppermute | solution.py:382

commit v4 on v3

--- a/solution.py
+++ b/solution.py
@@ -321,14 +321,14 @@
         if more:
             sums = sums + sums_ref[here, :]
         if last:
-            held_ref[here, :] = sums
+            held_ref[here, :] = sums.astype(BF16)
         else:
             out_ref[here, :] = sums
     if last:
-        finish(held_ref, high_ref, out_ref, ())
-
-
-def finish(sums_ref, high_ref, out_ref, more):
+        finish(held_ref, high_ref, out_ref)
+
+
+def finish(sums_ref, high_ref, out_ref):
     samples, wide = sums_ref.shape
     dets = out_ref.shape[0]
     rows = min(512, samples)
@@ -342,13 +342,11 @@
         here = slice(step * rows, (step + 1) * rows)
         kept = []
         for b, lane in enumerate(lanes):
-            part = sums_ref[here, b * LANES : (b + 1) * LANES].astype(BF16)
+            part = sums_ref[here, b * LANES : (b + 1) * LANES]
             kept.append(jnp.where(high_ref[here, :] == lane, part, jnp.zeros_like(part)))
         values = lax.dot_general(
             gather, jnp.concatenate(kept, axis=1), CONTRACT_LAST, preferred_element_type=F32
         )
-        for other in more:
-            values = values + other[:, here].astype(F32)
         out_ref[:, here] = values.astype(BF16)
 
 
@@ -367,7 +365,7 @@
         in_specs=[pl.BlockSpec(memory_space=pltpu.VMEM)] * len(operands),
         scratch_shapes=[
             pltpu.VMEM((sum(counts) * LANES, wide), BF16),
-            pltpu.VMEM((8 if dets is None else samples, wide), F32),
+            pltpu.VMEM((16 if dets is None else samples, wide), BF16),
         ],
         compiler_params=pltpu.CompilerParams(vmem_limit_bytes=16 * 2**20),
         name="pick_values",
@@ -453,9 +451,7 @@
     near_packet, _ = lax.optimization_barrier((near_packet, piece))
     near_x = unpack_samples(near_packet, samples)
     far_x = unpack_samples(got, samples)
-    gathered[1], near_x, far_x = lax.optimization_barrier(
-        (gathered[1], near_x, far_x)
-    )
+    gathered[1:], near_x, far_x = lax.optimization_barrier((gathered[1:], near_x, far_x))
     pieces = [piece] + gathered
     others = []
     for s in range(1, far):

time: 28.7 us -> 29.1 us (1.014)
  starting transfers between devices: 9.89 us -> 10.6 us
    ppermute x10, starting transfers between devices: 9.89 us -> 10.6 us  [swap(): return lax.ppermute(value, axis, [(i, i ^ step) for i in range(size)])]
  transfers between devices with their start and end apart: 10 -> 10, of which waited for: 5 -> 5; matrix products, arithmetic and copies ran while one was open for 0% -> 0% of each run, Pallas kernels for 14% -> 13%
where the time goes in v4:
time: 29.1 us; the launch traced here: 29 us
  starting transfers between devices  10.6 us (36%)
  waiting for transfers between devices  9.53 us (33%)
  Pallas kernels  7.91 us (27%)
  other arithmetic  0.65 us (2%)
    ppermute x10, starting transfers between devices, swap(): return lax.ppermute(value, axis, [(i, i ^ step) for i in range(size)])  10.6 us
    ppermute x10, waiting for transfers between devices, swap(): return lax.ppermute(value, axis, [(i, i ^ step) for i in range(size)])  9.53 us
    pallas_call x3, Pallas kernels, pick_values(): pl.pallas_call(functools.partial(pick_kernel, counts, first * 2 * FOLD *...  3.15 us
    pallas_call x1, Pallas kernels, band_sums(): pl.pallas_call(functools.partial(band_kernel, tiles_each, slots), out_sha...  1.58 us
    pallas_call x1, Pallas kernels, spread_samples(): pl.pallas_call(spread_kernel, out_shape=(packet, packet), in_specs=[pl.Bl...  1.51 us
    pallas_call x2, Pallas kernels, unpack_samples(): pl.pallas_call(unpack_kernel, out_shape=(jax.ShapeDtypeStruct((samples, F...  1.02 us
    transpose x1, other arithmetic, on_device(): return (values.astype(F32) + other.astype(F32)).astype(BF16).T  0.65 us
    pallas_call x1, Pallas kernels, cycle_coefs(): pl.pallas_call(cycle_kernel, out_shape=jax.ShapeDtypeStruct((LANES, rows...  0.64 us
  transfers between devices with their start and end apart: 10, of which 5 were waited for; matrix products, arithmetic and copies ran while one was open for 0% of the time, Pallas kernels for 13%

profile of v4, /device:TPU:0, one launch (start us, length us, event | category | flops | bytes accessed | tf_op | source)
XLA Modules:
  0.0 29.0 jit_solution(9129591567526498708)
XLA Ops:
  0.0 1.6 %band_sums.1 = (f32[32,1024]{1,0:T(8,128)S(1)}, bf16[32,1024]{1,0:T(8,128)(2,1)S(1)}, s32[8,256]{1,0:T(8,128)S(1)}, s32[16,128]{1,0:T(8,128)S(1)}) custom-call(s32[32,32]{1,0:T(8,128)} %index_ref.1, f32[32,32]{1,0:T(8,128)} %weight_ref.1, s32[16]{0:T(128)} %orders_ref.1, s32[16,128]{1,0:T(8,128)} %bitcast.8, s32[16,128]{1,0:T(8,128)} %bitcast.9, ...), custom_call_target="tpu_custom_call" | custom-call | flops 2147483648 | bytes 8388608 | tf_op jit(solution)/shard_map/band_sums/pallas_call | solution.py:94
  1.6 0.2 copy-done.1
  1.8 1.5 %spread_samples.1 = (bf16[1056,128]{1,0:T(8,128)(2,1)S(1)}, bf16[1056,128]{1,0:T(8,128)(2,1)S(1)}) custom-call(s32[8,256]{1,0:T(8,128)S(1)} %get-tuple-element.30.lanes_ref, s32[16,128]{1,0:T(8,128)S(1)} %get-tuple-element.31.code_ref, bf16[2048,512]{1,0:T(8,128)(2,1)S(1)} %copy-done.1), custom_call_target="tpu_custom_call" | custom-call | flops 2147483648 | bytes 4194304 | tf_op jit(solution)/shard_map/spread_samples/pallas_call | solution.py:231
  3.3 3.1 %collective-permute-start.3 = (bf16[1056,128]{1,0:T(8,128)(2,1)S(1)}, bf16[1056,128]{1,0:T(8,128)(2,1)S(1)}, u32[]{:S(2)}, u32[]{:S(2)}) collective-permute-start(bf16[1056,128]{1,0:T(8,128)(2,1)S(1)} %get-tuple-element.39), channel_id=1, source_target_pairs={{0,2},{1,3},{2,0},{3,1},{4,6},{5,7},{6,4},{7,5},{8,10},{9,11},{10,... | collective-permute-start | bytes 811016 | tf_op jit(solution)/shard_map/ppermute | solution.py:380
  6.4 1.5 %collective-permute-start = (bf16[32,1024]{1,0:T(8,128)(2,1)S(1)}, bf16[32,1024]{1,0:T(8,128)(2,1)S(1)}, u32[]{:S(2)}, u32[]{:S(2)}) collective-permute-start(bf16[32,1024]{1,0:T(8,128)(2,1)S(1)} %get-tuple-element.29), channel_id=1, source_target_pairs={{0,16},{16,0},{1,17},{17,1},{2,18},{18,2},{3,19},{19,3},{4,20},{20... | collective-permute-start | bytes 196616 | tf_op jit(solution)/shard_map/ppermute | solution.py:380
  7.9 2.8 %collective-permute-done.recv_ref = bf16[32,1024]{1,0:T(8,128)(2,1)S(1)} collective-permute-done((bf16[32,1024]{1,0:T(8,128)(2,1)S(1)}, bf16[32,1024]{1,0:T(8,128)(2,1)S(1)}, u32[]{:S(2)}, u32[]{:S(2)}) %collective-permute-start) | collective-permute-done | bytes 65568 | tf_op jit(solution)/shard_map/ppermute | solution.py:380
  10.7 0.6 %cycle_coefs.1.refs_0_ = bf16[128,256]{1,0:T(8,128)(2,1)S(1)} custom-call(f32[32,1024]{1,0:T(8,128)S(1)} %get-tuple-element.28.own_ref, bf16[32,1024]{1,0:T(8,128)(2,1)S(1)} %collective-permute-done.recv_ref, bf16[1024,1024]{1,0:T(8,128)(2,1)S(1)} %bitcast.6), custom_call_target="tpu_custom_call" | custom-call | tf_op jit(solution)/shard_map/cycle_coefs/pallas_call | solution.py:142
  11.3 1.6 %collective-permute-start.4 = (bf16[128,256]{1,0:T(8,128)(2,1)S(1)}, bf16[128,256]{1,0:T(8,128)(2,1)S(1)}, u32[]{:S(2)}, u32[]{:S(2)}) collective-permute-start(bf16[128,256]{1,0:T(8,128)(2,1)S(1)} %cycle_coefs.1.refs_0_), channel_id=1, source_target_pairs={{0,4},{4,0},{8,12},{12,8},{1,5},{5,1},{9,13},{13,9},{2,6},{6,2},{1... | collective-permute-start | bytes 196616 | tf_op jit(solution)/shard_map/ppermute | solution.py:380
  12.9 2.6 %collective-permute-start.1 = (bf16[128,256]{1,0:T(8,128)(2,1)S(1)}, bf16[128,256]{1,0:T(8,128)(2,1)S(1)}, u32[]{:S(2)}, u32[]{:S(2)}) collective-permute-start(bf16[128,256]{1,0:T(8,128)(2,1)S(1)} %cycle_coefs.1.refs_0_), channel_id=1, source_target_pairs={{0,8},{4,12},{8,0},{12,4},{1,9},{5,13},{9,1},{13,5},{2,10},{6,14},... | collective-permute-start | bytes 196616 | tf_op jit(solution)/shard_map/ppermute | solution.py:380
  15.5 0.2 collective-permute-start.2
  15.8 0.5 %unpack_samples.2 = (bf16[2048,256]{1,0:T(8,128)(2,1)S(1)}, bf16[2048,128]{1,0:T(8,128)(2,1)S(1)}, bf16[2048,128]{1,0:T(8,128)(2,1)S(1)}) custom-call(bf16[1056,128]{1,0:T(8,128)(2,1)S(1)} %get-tuple-element.35.packet_ref), custom_call_target="tpu_custom_call" | custom-call | flops 268435456 | bytes 2097152 | tf_op jit(solution)/shard_map/unpack_samples/pallas_call | solution.py:271
  16.3 0.6 %collective-permute-start.6 = (bf16[128,256]{1,0:T(8,128)(2,1)S(1)}, bf16[128,256]{1,0:T(8,128)(2,1)S(1)}, u32[]{:S(2)}, u32[]{:S(2)}) collective-permute-start(bf16[128,256]{1,0:T(8,128)(2,1)S(1)} %collective-permute-done.4.refs_1_), channel_id=1, source_target_pairs={{0,1},{1,0},{2,3},{3,2},{4,5},{5,4},{6,7},{7,6},{8,9},{9,8},{10,11... | collective-permute-start | bytes 196616 | tf_op jit(solution)/shard_map/ppermute | solution.py:380
  16.9 0.5 %unpack_samples.3 = (bf16[2048,256]{1,0:T(8,128)(2,1)S(1)}, bf16[2048,128]{1,0:T(8,128)(2,1)S(1)}, bf16[2048,128]{1,0:T(8,128)(2,1)S(1)}) custom-call(bf16[1056,128]{1,0:T(8,128)(2,1)S(1)} %collective-permute-done.3.packet_ref), custom_call_target="tpu_custom_call" | custom-call | flops 268435456 | bytes 2097152 | tf_op jit(solution)/shard_map/unpack_samples/pallas_call | solution.py:271
  17.4 2.1 %collective-permute-done.1.refs_2_ = bf16[128,256]{1,0:T(8,128)(2,1)S(1)} collective-permute-done((bf16[128,256]{1,0:T(8,128)(2,1)S(1)}, bf16[128,256]{1,0:T(8,128)(2,1)S(1)}, u32[]{:S(2)}, u32[]{:S(2)}) %collective-permute-start.1) | collective-permute-done | bytes 65568 | tf_op jit(solution)/shard_map/ppermute | solution.py:380
  19.5 2.1 %collective-permute-done.2.refs_3_ = bf16[128,256]{1,0:T(8,128)(2,1)S(1)} collective-permute-done((bf16[128,256]{1,0:T(8,128)(2,1)S(1)}, bf16[128,256]{1,0:T(8,128)(2,1)S(1)}, u32[]{:S(2)}, u32[]{:S(2)}) %collective-permute-start.2) | collective-permute-done | bytes 65568 | tf_op jit(solution)/shard_map/ppermute | solution.py:380
  21.6 0.5 %collective-permute-start.8 = (bf16[128,256]{1,0:T(8,128)(2,1)S(1)}, bf16[128,256]{1,0:T(8,128)(2,1)S(1)}, u32[]{:S(2)}, u32[]{:S(2)}) collective-permute-start(bf16[128,256]{1,0:T(8,128)(2,1)S(1)} %collective-permute-done.2.refs_3_), channel_id=1, source_target_pairs={{0,1},{1,0},{2,3},{3,2},{4,5},{5,4},{6,7},{7,6},{8,9},{9,8},{10,11... | collective-permute-start | bytes 196616 | tf_op jit(solution)/shard_map/ppermute | solution.py:380
  22.1 0.7 %pick_values.4.refs_4_ = f32[2048,256]{1,0:T(8,128)S(1)} custom-call(bf16[2048,256]{1,0:T(8,128)(2,1)S(1)} %get-tuple-element.48.x_ref, bf16[2048,128]{1,0:T(8,128)(2,1)S(1)} %get-tuple-element.49.low_ref, bf16[2048,128]{1,0:T(8,128)(2,1)S(1)} %get-tuple-element.50.high_ref, bf16[128,256]{1,0:T(8,128)(2,1)S(1)} %cycle_coefs.1.refs_0_, ...), custom_call_target="tpu_custom_call" | custom-call | flops 536870912 | bytes 4194304 | tf_op jit(solution)/shard_map/pick_values/pallas_call | solution.py:360
  22.9 0.0 collective-permute-done.7.refs_6_.refs_2_
  22.9 0.2 collective-permute-done.8.refs_7_.refs_3_
  23.0 1.0 %pick_values.5 = bf16[16,2048]{1,0:T(8,128)(2,1)S(1)} custom-call(bf16[2048,256]{1,0:T(8,128)(2,1)S(1)} %get-tuple-element.48.x_ref, bf16[2048,128]{1,0:T(8,128)(2,1)S(1)} %get-tuple-element.49.low_ref, bf16[2048,128]{1,0:T(8,128)(2,1)S(1)} %get-tuple-element.50.high_ref, bf16[128,256]{1,0:T(8,128)(2,1)S(1)} %collective-permute-done.5.refs_4_.refs_0_, ...), custom_call_target="tpu_custom_call" | custom-call | flops 536870912 | bytes 4194304 | tf_op jit(solution)/shard_map/pick_values/pallas_call | solution.py:360
  24.0 0.5 %collective-permute-start.9 = (bf16[16,2048]{1,0:T(8,128)(2,1)S(1)}, bf16[16,2048]{1,0:T(8,128)(2,1)S(1)}, u32[]{:S(2)}, u32[]{:S(2)}) collective-permute-start(bf16[16,2048]{1,0:T(8,128)(2,1)S(1)} %pick_values.5), channel_id=1, source_target_pairs={{0,2},{1,3},{2,0},{3,1},{4,6},{5,7},{6,4},{7,5},{8,10},{9,11},{10,... | collective-permute-start | bytes 196616 | tf_op jit(solution)/shard_map/ppermute | solution.py:380
  24.5 1.5 %pick_values.3 = bf16[16,2048]{1,0:T(8,128)(2,1)S(1)} custom-call(bf16[2048,256]{1,0:T(8,128)(2,1)S(1)} %get-tuple-element.43.x_ref, bf16[2048,128]{1,0:T(8,128)(2,1)S(1)} %get-tuple-element.44.low_ref, bf16[2048,128]{1,0:T(8,128)(2,1)S(1)} %get-tuple-element.45.high_ref, bf16[128,256]{1,0:T(8,128)(2,1)S(1)} %cycle_coefs.1.refs_0_, ...), custom_call_target="tpu_custom_call" | custom-call | flops 1073741824 | bytes 4194304 | tf_op jit(solution)/shard_map/pick_values/pallas_call | solution.py:360
  26.0 2.4 %collective-permute-done.9 = bf16[16,2048]{1,0:T(8,128)(2,1)S(1)} collective-permute-done((bf16[16,2048]{1,0:T(8,128)(2,1)S(1)}, bf16[16,2048]{1,0:T(8,128)(2,1)S(1)}, u32[]{:S(2)}, u32[]{:S(2)}) %collective-permute-start.9) | collective-permute-done | bytes 65568 | tf_op jit(solution)/shard_map/ppermute | solution.py:380
  28.3 0.6 %fusion = bf16[2048,16]{0,1:T(8,128)(2,1)} fusion(bf16[16,2048]{1,0:T(8,128)(2,1)S(1)} %collective-permute-done.9, bf16[16,2048]{1,0:T(8,128)(2,1)S(1)} %pick_values.3), kind=kLoop, calls=%fused_computation.1 | loop fusion | flops 131072 | bytes 196608 | tf_op jit(solution)/shard_map/transpose | solution.py:464
  (9 shorter events, 0.0 us)
Async XLA Ops:
  0.0 1.8 %copy-start.1 = (bf16[2048,512]{1,0:T(8,128)(2,1)S(1)}, bf16[2048,512]{1,0:T(8,128)(2,1)}, u32[]{:S(2)}) copy-start(bf16[2048,512]{1,0:T(8,128)(2,1)} %interp_ref.1) | copy-start | bytes 6291460
  1.8 8.8 %copy-start = (bf16[1,1024,1024]{2,1,0:T(8,128)(2,1)S(1)}, bf16[1,1024,1024]{2,1,0:T(8,128)(2,1)}, u32[]{:S(2)}) copy-start(bf16[1,1024,1024]{2,1,0:T(8,128)(2,1)} %param.11) | copy-start | bytes 6291460
  3.3 13.5 %collective-permute-start.3 = (bf16[1056,128]{1,0:T(8,128)(2,1)S(1)}, bf16[1056,128]{1,0:T(8,128)(2,1)S(1)}, u32[]{:S(2)}, u32[]{:S(2)}) collective-permute-start(bf16[1056,128]{1,0:T(8,128)(2,1)S(1)} %get-tuple-element.39), channel_id=1, source_target_pairs={{0,2},{1,3},{2,0},{3,1},{4,6},{5,7},{6,4},{7,5},{8,10},{9,11},{10,... | collective-permute-start | bytes 811016 | tf_op jit(solution)/shard_map/ppermute | solution.py:380
  6.4 4.3 %collective-permute-start = (bf16[32,1024]{1,0:T(8,128)(2,1)S(1)}, bf16[32,1024]{1,0:T(8,128)(2,1)S(1)}, u32[]{:S(2)}, u32[]{:S(2)}) collective-permute-start(bf16[32,1024]{1,0:T(8,128)(2,1)S(1)} %get-tuple-element.29), channel_id=1, source_target_pairs={{0,16},{16,0},{1,17},{17,1},{2,18},{18,2},{3,19},{19,3},{4,20},{20... | collective-permute-start | bytes 196616 | tf_op jit(solution)/shard_map/ppermute | solution.py:380
  11.3 5.0 %collective-permute-start.4 = (bf16[128,256]{1,0:T(8,128)(2,1)S(1)}, bf16[128,256]{1,0:T(8,128)(2,1)S(1)}, u32[]{:S(2)}, u32[]{:S(2)}) collective-permute-start(bf16[128,256]{1,0:T(8,128)(2,1)S(1)} %cycle_coefs.1.refs_0_), channel_id=1, source_target_pairs={{0,4},{4,0},{8,12},{12,8},{1,5},{5,1},{9,13},{13,9},{2,6},{6,2},{1... | collective-permute-start | bytes 196616 | tf_op jit(solution)/shard_map/ppermute | solution.py:380
  12.9 6.6 %collective-permute-start.1 = (bf16[128,256]{1,0:T(8,128)(2,1)S(1)}, bf16[128,256]{1,0:T(8,128)(2,1)S(1)}, u32[]{:S(2)}, u32[]{:S(2)}) collective-permute-start(bf16[128,256]{1,0:T(8,128)(2,1)S(1)} %cycle_coefs.1.refs_0_), channel_id=1, source_target_pairs={{0,8},{4,12},{8,0},{12,4},{1,9},{5,13},{9,1},{13,5},{2,10},{6,14},... | collective-permute-start | bytes 196616 | tf_op jit(solution)/shard_map/ppermute | solution.py:380
  15.5 6.1 %collective-permute-start.2 = (bf16[128,256]{1,0:T(8,128)(2,1)S(1)}, bf16[128,256]{1,0:T(8,128)(2,1)S(1)}, u32[]{:S(2)}, u32[]{:S(2)}) collective-permute-start(bf16[128,256]{1,0:T(8,128)(2,1)S(1)} %cycle_coefs.1.refs_0_), channel_id=1, source_target_pairs={{0,12},{4,8},{8,4},{12,0},{1,13},{5,9},{9,5},{13,1},{2,14},{6,10},... | collective-permute-start | bytes 196616 | tf_op jit(solution)/shard_map/ppermute | solution.py:380
  15.8 7.1 %collective-permute-start.5 = (bf16[128,256]{1,0:T(8,128)(2,1)S(1)}, bf16[128,256]{1,0:T(8,128)(2,1)S(1)}, u32[]{:S(2)}, u32[]{:S(2)}) collective-permute-start(bf16[128,256]{1,0:T(8,128)(2,1)S(1)} %cycle_coefs.1.refs_0_), channel_id=1, source_target_pairs={{0,1},{1,0},{2,3},{3,2},{4,5},{5,4},{6,7},{7,6},{8,9},{9,8},{10,11... | collective-permute-start | bytes 196616 | tf_op jit(solution)/shard_map/ppermute | solution.py:380
  16.3 6.6 %collective-permute-start.6 = (bf16[128,256]{1,0:T(8,128)(2,1)S(1)}, bf16[128,256]{1,0:T(8,128)(2,1)S(1)}, u32[]{:S(2)}, u32[]{:S(2)}) collective-permute-start(bf16[128,256]{1,0:T(8,128)(2,1)S(1)} %collective-permute-done.4.refs_1_), channel_id=1, source_target_pairs={{0,1},{1,0},{2,3},{3,2},{4,5},{5,4},{6,7},{7,6},{8,9},{9,8},{10,11... | collective-permute-start | bytes 196616 | tf_op jit(solution)/shard_map/ppermute | solution.py:380
  21.6 1.3 %collective-permute-start.7 = (bf16[128,256]{1,0:T(8,128)(2,1)S(1)}, bf16[128,256]{1,0:T(8,128)(2,1)S(1)}, u32[]{:S(2)}, u32[]{:S(2)}) collective-permute-start(bf16[128,256]{1,0:T(8,128)(2,1)S(1)} %collective-permute-done.1.refs_2_), channel_id=1, source_target_pairs={{0,1},{1,0},{2,3},{3,2},{4,5},{5,4},{6,7},{7,6},{8,9},{9,8},{10,11... | collective-permute-start | bytes 196616 | tf_op jit(solution)/shard_map/ppermute | solution.py:380
  21.6 1.4 %collective-permute-start.8 = (bf16[128,256]{1,0:T(8,128)(2,1)S(1)}, bf16[128,256]{1,0:T(8,128)(2,1)S(1)}, u32[]{:S(2)}, u32[]{:S(2)}) collective-permute-start(bf16[128,256]{1,0:T(8,128)(2,1)S(1)} %collective-permute-done.2.refs_3_), channel_id=1, source_target_pairs={{0,1},{1,0},{2,3},{3,2},{4,5},{5,4},{6,7},{7,6},{8,9},{9,8},{10,11... | collective-permute-start | bytes 196616 | tf_op jit(solution)/shard_map/ppermute | solution.py:380
  24.0 4.4 %collective-permute-start.9 = (bf16[16,2048]{1,0:T(8,128)(2,1)S(1)}, bf16[16,2048]{1,0:T(8,128)(2,1)S(1)}, u32[]{:S(2)}, u32[]{:S(2)}) collective-permute-start(bf16[16,2048]{1,0:T(8,128)(2,1)S(1)} %pick_values.5), channel_id=1, source_target_pairs={{0,2},{1,3},{2,0},{3,1},{4,6},{5,7},{6,4},{7,5},{8,10},{9,11},{10,... | collective-permute-start | bytes 196616 | tf_op jit(solution)/shard_map/ppermute | solution.py:380
